TPU v7x, 32 devices: a whole 2x2x4 slice. The times are simulated.
32 devices in a mesh: ga: 2 (over x), col: 16 (over z, y, core).
Axes of the slice: x: 2, y: 2, z: 4, core: 2. Of those that a mesh axis runs over, the one named last changes fastest.
Arguments:
- cholesky: bfloat16 [1024, 1024, 512], P(('ga', 'col')), parts along dimension 0, may hold values from -0.1875 to 0.1875
- amplitudes: bfloat16 [512, 512, 512], P('ga', 'col'), parts along dimension 0, may hold values from -0.25 to 0.25
Outputs:
- ladder: float32 [512, 2, 512], P('ga', None, 'col'), parts along dimension 0
There are 2 independent parts, one for each index of `ga`. A program takes and returns all parts, laid end to end along the dimension named above; each array names one. Nothing has to cross between parts.
All inputs are finite; a program needn't handle non-finite values.
Results may differ from a plain program's by a relative error of at most 0.0029.
Values may be sent and summed in bfloat16 or wider, within the bound.
No kernel may reach another device: no remote copies, remote signals or barrier semaphores. Data moves between devices by JAX's collectives and lax.ppermute only.
A program may use at most 128 MiB of HBM per device.

v0:
```python
import jax
import jax.numpy as jnp
from jax import lax
from jax.sharding import PartitionSpec as P

A_WIN = 2


def shards(cholesky, amplitudes):
    window_local = jnp.transpose(cholesky[:, :, :A_WIN], (0, 2, 1))
    gathered = lax.all_gather(window_local, "col", axis=0, tiled=True)
    integrals = jnp.einsum(
        "clb,dal->acbd", cholesky, gathered, preferred_element_type=jnp.float32
    ).astype(jnp.bfloat16)
    partial_value = jnp.einsum(
        "pcd,acbd->pab", amplitudes, integrals, preferred_element_type=jnp.float32
    )
    return lax.psum_scatter(partial_value, "col", scatter_dimension=2, tiled=True)


def solution(mesh):
    in_specs = (P(("ga", "col"), None, None), P("ga", "col", None))
    out_specs = P("ga", None, "col")
    return jax.shard_map(shards, mesh=mesh, in_specs=in_specs, out_specs=out_specs, check_vma=False)
```

profile of v0, /device:TPU:0, one launch (start us, length us, event | category | flops | bytes accessed | tf_op | source)
XLA Modules:
  0.0 194.5 jit_solution(14769614902014618479)
XLA Ops:
  6.5 0.0 all-gather.2.cloned.1.call-start
  6.5 7.5 %slice.3 = bf16[32,1024,2]{2,1,0:T(8,128)(2,1)} slice(bf16[32,1024,512]{2,1,0:T(8,128)(2,1)} %param.2), slice={[0:32], [0:1024], [0:2]} | slice | bytes 262144 | tf_op jit(solution)/shard_map/slice | solution.py:10
  14.0 7.0 %copy.8 = bf16[32,1024,2]{1,2,0:T(2,128)(2,1)} copy(bf16[32,1024,2]{2,1,0:T(8,128)(2,1)} %slice.3) | data formatting | bytes 262144
  21.0 0.0 all-gather.2.cloned.1.call-update
  21.0 0.0 reduce-scatter.2.cloned.1.call-start
  21.1 44.3 %all-gather.2.cloned.1.call-done = bf16[512,2,1024]{2,1,0:T(2,128)(2,1)} async-done(((bf16[32,2,1024]{2,1,0:T(2,128)(2,1)}), bf16[512,2,1024]{2,1,0:T(2,128)(2,1)}) %all-gather.2.cloned.1.call-update) | async-done | bytes 2097168 | tf_op jit(solution)/shard_map/all_gather | solution.py:11
  65.4 43.2 %fusion.31 = bf16[2,32,512,512]{3,2,1,0:T(8,128)(2,1)} fusion(bf16[32,1024,512]{2,1,0:T(8,128)(2,1)} %param.2, bf16[512,2,1024,1]{2,1,0,3:T(2,128)(2,1)} %bitcast.36), kind=kOutput, calls=%fused_computation.1.clone.clone.clone.1 | convolution fusion | flops 34376515584 | bytes 69206016 | tf_op jit(solution)/shard_map/clb,dal->acbd/dot_general | solution.py:12
  108.5 22.7 %fusion.13 = f32[256,2,512]{0,2,1:T(8,128)} fusion(bf16[256,32,512]{2,1,0:T(8,128)(2,1)} %param.3, bf16[2,32,512,512]{3,2,1,0:T(8,128)(2,1)} %fusion.31), kind=kOutput, calls=%fused_computation.8 | convolution fusion | flops 8589934592 | bytes 42991616 | tf_op jit(solution)/shard_map/pcd,acbd->pab/dot_general | solution.py:15
  131.2 0.0 reduce-scatter.2.cloned.1.call-update
  131.2 56.4 %reduce-scatter.2.cloned.1.call-done = f32[256,2,32]{0,2,1:T(8,128)} async-done(((f32[256,2,512]{0,2,1:T(8,128)}), f32[256,2,32]{0,2,1:T(8,128)}) %reduce-scatter.2.cloned.1.call-update) | async-done | bytes 65552 | tf_op jit(solution)/shard_map/reduce_scatter | solution.py:18
Async XLA Ops:
  6.5 58.8 %all-gather.2.cloned.1.call-start = ((), (), s32[]{:S(2)}) async-start(), calls=%async_computation.1 | async-start | bytes 2228224 | tf_op jit(solution)/shard_map/all_gather | solution.py:11
  21.0 166.6 %reduce-scatter.2.cloned.1.call-start = ((), (), s32[]{:S(2)}) async-start(), calls=%async_computation.2 | async-start | bytes 1114112 | tf_op jit(solution)/shard_map/reduce_scatter | solution.py:18
Sparse Core Ops, SparseCore 0:
  21.2 44.1 all-gather.1
  131.4 56.2 reduce-scatter.1
where the time goes:
time: 195 us; the launch traced here: 194 us
  waiting for transfers between devices  101 us (52%)
  matrix products  65.8 us (34%)
  local copies, waits for them, and re-layouts  14.5 us (7%)
  between operations  13.4 us (7%)
    reduce_scatter x1, waiting for transfers between devices, shards(): lax.psum_scatter(partial_value, 'col', scatter_dimension=2, tiled=True)  56.4 us
    all_gather x1, waiting for transfers between devices, shards(): gathered = lax.all_gather(window_local, 'col', axis=0, tiled=True)  44.3 us
    dot_general x1, matrix products, shards(): jnp.einsum('clb,dal->acbd', cholesky, gathered, preferred_element_type=jn...  43.2 us
    dot_general x1, matrix products, shards(): jnp.einsum('pcd,acbd->pab', amplitudes, integrals, preferred_element_type...  22.7 us
    slice x1, local copies, waits for them, and re-layouts, shards(): window_local = jnp.transpose(cholesky[:, :, :A_WIN], (0, 2, 1))  7.51 us
    unnamed x1, local copies, waits for them, and re-layouts  6.97 us
  transfers between devices with their start and end apart: 2, of which 2 were waited for; matrix products, arithmetic and copies ran while one was open for 0% of the time, Pallas kernels for 0%

commit v1 on v0

v1 whole, which is shorter than its diff:
```python
import functools

import jax
import jax.numpy as jnp
from jax import lax
from jax.experimental import pallas as pl
from jax.experimental.pallas import tpu as pltpu
from jax.sharding import PartitionSpec as P


A_WIN = 2
CORES = 2
LANES = 128
MIB = 1 << 20
GROUP = 8
GRANT = 48 * MIB


def ring_order(chips):
    return list(range(0, chips, 2)) + list(range(1, chips, 2))[::-1]


def window_kernel(chol_ref, out_ref, rows, pick, arrived):
    own, depth, _ = rows.shape
    chunk = depth // arrived.shape[0]
    copies = []
    for i in range(depth // chunk):
        here = pl.ds(i * chunk, chunk)
        copies.append(
            pltpu.make_async_copy(chol_ref.at[:, here, pl.ds(0, LANES)], rows.at[:, here, :], arrived.at[i])
        )
        copies[i].start()
    source = lax.broadcasted_iota(jnp.int32, (LANES, LANES), 0)
    target = lax.broadcasted_iota(jnp.int32, (LANES, LANES), 1)
    for row in range(own):
        hit = source * own + row == target
        pick[row * LANES : (row + 1) * LANES, :] = jnp.where(hit & (source < A_WIN), 1.0, 0.0).astype(pick.dtype)
    for i in range(depth // chunk):
        here = slice(i * chunk, (i + 1) * chunk)
        copies[i].wait()
        wide = jnp.concatenate([rows[row, here, :] for row in range(own)], axis=1)
        picked = jnp.dot(wide, pick[...], preferred_element_type=jnp.float32)
        turned = jnp.transpose(picked)
        for a in range(A_WIN):
            out_ref[a, :, here] = turned[a * own : (a + 1) * own].astype(out_ref.dtype)


def window_of(cholesky):
    own, depth, _ = cholesky.shape
    return pl.pallas_call(
        window_kernel,
        out_shape=jax.ShapeDtypeStruct((A_WIN, own, depth), cholesky.dtype),
        in_specs=[pl.BlockSpec(memory_space=pltpu.HBM)],
        out_specs=pl.BlockSpec(memory_space=pltpu.VMEM),
        scratch_shapes=[
            pltpu.VMEM((own, depth, LANES), cholesky.dtype),
            pltpu.VMEM((own * LANES, LANES), cholesky.dtype),
            pltpu.SemaphoreType.DMA((4,)),
        ],
        cost_estimate=pl.CostEstimate(flops=0, bytes_accessed=2 * own * depth * LANES, transcendentals=0),
        compiler_params=pltpu.CompilerParams(vmem_limit_bytes=GRANT),
        name="window",
    )(cholesky)


def turn_kernel(amp_ref, *refs, first):
    out_ref, taken, given, flat, arrived, left = refs[-6:]
    chunks, rows, tile, orbitals = taken.shape
    steps = pl.ds(first, tile)
    comes, goes = [], []
    for i in range(chunks):
        here = pl.ds(i * rows, rows)
        comes.append(pltpu.make_async_copy(amp_ref.at[here, steps, :], taken.at[i], arrived.at[i]))
        goes.append(pltpu.make_async_copy(given.at[i], out_ref.at[steps, here, :], left.at[i]))
        comes[i].start()
    for i in range(chunks):
        comes[i].wait()
        for at in range(0, orbitals, LANES):
            lanes = at // LANES
            flat[lanes] = taken[i, :, :, at : at + LANES].astype(jnp.float32).reshape(rows * tile, LANES)
            for c in range(tile):
                given[i, c, :, at : at + LANES] = flat[lanes, pl.ds(c, rows, stride=tile), :].astype(given.dtype)
        goes[i].start()
    for copy in goes:
        copy.wait()


def turn(amplitudes, part, parts, held):
    pairs, steps, orbitals = amplitudes.shape
    tile = max(steps // parts, min(8, steps))
    rows = min(64, pairs)
    chunks = pairs // rows
    if part * tile >= steps:
        return held
    extra = [] if held is None else [held]
    return pl.pallas_call(
        functools.partial(turn_kernel, first=part * tile),
        out_shape=jax.ShapeDtypeStruct((steps, pairs, orbitals), amplitudes.dtype),
        in_specs=[pl.BlockSpec(memory_space=pltpu.HBM)] * (1 + len(extra)),
        out_specs=pl.BlockSpec(memory_space=pltpu.HBM),
        scratch_shapes=[
            pltpu.VMEM((chunks, rows, tile, orbitals), amplitudes.dtype),
            pltpu.VMEM((chunks, tile, rows, orbitals), amplitudes.dtype),
            pltpu.VMEM((orbitals // LANES, rows * tile, LANES), jnp.float32),
            pltpu.SemaphoreType.DMA((chunks,)),
            pltpu.SemaphoreType.DMA((chunks,)),
        ],
        input_output_aliases={1: 0} if extra else {},
        cost_estimate=pl.CostEstimate(flops=0, bytes_accessed=4 * tile * pairs * orbitals, transcendentals=0),
        compiler_params=pltpu.CompilerParams(vmem_limit_bytes=GRANT),
        name="turn",
    )(amplitudes, *extra)


def ladder_kernel(order_ref, *refs, pieces, group):
    piece_refs = refs[:pieces]
    amp_ref, chol_ref, keep_ref, send_ref, window, amps, chols, half, total, came, amp_came, chol_came = refs[pieces:]
    own = piece_refs[0].shape[1]
    steps, pairs, _ = amp_ref.shape
    groups = steps // group

    def fetch(g, slot, c):
        at = g * group + c
        return (
            pltpu.make_async_copy(amp_ref.at[at], amps.at[slot, c], amp_came.at[slot, c]),
            pltpu.make_async_copy(chol_ref.at[at], chols.at[slot, c], chol_came.at[slot, c]),
        )

    gathered = []
    for i in range(pieces):
        start = pl.multiple_of(order_ref[i] * own, own)
        gathered.append(pltpu.make_async_copy(piece_refs[i], window.at[:, pl.ds(start, own), :], came.at[i]))
        gathered[i].start()
    for c in range(group):
        for copy in fetch(0, 0, c):
            copy.start()
    total[...] = jnp.zeros_like(total)
    for copy in gathered:
        copy.wait()

    def advance(g, _):
        slot = lax.rem(g, 2)

        @pl.when(g + 1 < groups)
        def _():
            for c in range(group):
                for copy in fetch(g + 1, 1 - slot, c):
                    copy.start()

        for c in range(group):
            for copy in fetch(g, slot, c):
                copy.wait()
            for a in range(A_WIN):
                half[c, a * pairs : (a + 1) * pairs, :] = jnp.dot(
                    amps[slot, c], window[a], preferred_element_type=jnp.float32
                ).astype(half.dtype)
            total[...] += jnp.dot(half[c], chols[slot, c], preferred_element_type=jnp.float32)
        return 0

    lax.fori_loop(0, groups, advance, 0)
    core = order_ref[pieces]
    chips, _, width, _ = keep_ref.shape
    for a in range(A_WIN):
        turned = jnp.transpose(total[a * pairs : (a + 1) * pairs, :])
        total_t = turned.reshape(chips, CORES, width, pairs)
        first, second = total_t[:, 0], total_t[:, 1]
        keep_ref[:, a] = jnp.where(core == 0, first, second)
        send_ref[:, a] = jnp.where(core == 0, second, first)


def ladder_of(order, pieces, amplitudes, cholesky, chips):
    steps, pairs, orbitals = amplitudes.shape
    _, depth, _ = cholesky.shape
    group = GROUP if steps % GROUP == 0 else 1
    width = orbitals // (chips * CORES)
    shape = jax.ShapeDtypeStruct((chips, A_WIN, width, pairs), jnp.float32)
    flops = 2 * steps * pairs * A_WIN * orbitals * depth * 2
    kind = amplitudes.dtype
    return pl.pallas_call(
        functools.partial(ladder_kernel, pieces=len(pieces), group=group),
        out_shape=(shape, shape),
        in_specs=[pl.BlockSpec(memory_space=pltpu.SMEM)]
        + [pl.BlockSpec(memory_space=pl.ANY)] * len(pieces)
        + [pl.BlockSpec(memory_space=pltpu.HBM)] * 2,
        out_specs=[pl.BlockSpec(memory_space=pltpu.VMEM)] * 2,
        scratch_shapes=[
            pltpu.VMEM((A_WIN, orbitals, depth), kind),
            pltpu.VMEM((2, group, pairs, orbitals), kind),
            pltpu.VMEM((2, group, depth, orbitals), kind),
            pltpu.VMEM((group, A_WIN * pairs, depth), kind),
            pltpu.VMEM((A_WIN * pairs, orbitals), jnp.float32),
            pltpu.SemaphoreType.DMA((len(pieces),)),
            pltpu.SemaphoreType.DMA((2, group)),
            pltpu.SemaphoreType.DMA((2, group)),
        ],
        cost_estimate=pl.CostEstimate(
            flops=flops, bytes_accessed=2 * (cholesky.size + amplitudes.size), transcendentals=0
        ),
        compiler_params=pltpu.CompilerParams(vmem_limit_bytes=GRANT),
        name="ladder",
    )(order, *pieces, amplitudes, cholesky)


def shards(cholesky, amplitudes, *, devices):
    return part(cholesky, amplitudes, devices)


def part(cholesky, amplitudes, devices):
    chips = devices // CORES
    ring = ring_order(chips)
    place = [ring.index(chip) for chip in range(chips)]
    me = lax.axis_index("col")
    core = me % CORES

    def along(step):
        return [
            (ring[i] * CORES + c, ring[(i + step) % chips] * CORES + c) for i in range(chips) for c in range(CORES)
        ]

    partner = [(i, i ^ 1) for i in range(devices)]
    window = window_of(cholesky)

    def hop(piece, step):
        return lax.ppermute(piece, "col", along(step))

    mine = [(0, window)]
    ahead = back = window
    by_step = None
    hops = chips // 2
    for at_hop in range(1, hops + 1):
        ahead = hop(ahead, 1)
        mine.append((-at_hop, ahead))
        if at_hop < hops:
            back = hop(back, -1)
            mine.append((at_hop, back))
        by_step = turn(amplitudes, at_hop - 1, hops, by_step)
    theirs = [(far, lax.ppermute(piece, "col", partner)) for far, piece in mine]

    at = sum(jnp.where(me // CORES == chip, place[chip], 0) for chip in range(chips))

    def owner(away):
        where = (at + away) % chips
        return sum(jnp.where(where == i, ring[i], 0) for i in range(chips))

    order = jnp.stack(
        [owner(far) * CORES + core for far, _ in mine]
        + [owner(far) * CORES + 1 - core for far, _ in theirs]
        + [core]
    ).astype(jnp.int32)
    pieces = [piece for _, piece in mine + theirs]
    keep, send = ladder_of(order, pieces, by_step, cholesky, chips)
    summed = keep + lax.ppermute(send, "col", partner)
    groups = [[chip * CORES + c for chip in range(chips)] for c in range(CORES)]
    parts = lax.all_to_all(summed, "col", 0, 0, tiled=True, axis_index_groups=groups)
    return jnp.transpose(parts.sum(0), (2, 0, 1))


def solution(mesh):
    in_specs = (P(("ga", "col"), None, None), P("ga", "col", None))
    out_specs = P("ga", None, "col")
    devices = mesh.shape["col"]
    body = functools.partial(shards, devices=devices)
    return jax.shard_map(body, mesh=mesh, in_specs=in_specs, out_specs=out_specs, check_vma=False)
```

time: 195 us -> 104 us (0.53)
  waiting for transfers between devices: 101 us -> 12.9 us
  matrix products: 65.8 us -> 0 us
  Pallas kernels: 0 us -> 58.1 us
  blocking collectives: 0 us -> 20.9 us
  local copies, waits for them, and re-layouts: 14.5 us -> 0.1 us
  between operations: 13.4 us -> 0.11 us
  starting transfers between devices: 0.04 us -> 10.6 us
    dot_general x2 -> x0, matrix products: 65.8 us -> none  [the longest x1 43.2 us: shards(): jnp.einsum('clb,dal->acbd', cholesky, gathered, preferred_element_type=jn...]
    pallas_call x0 -> x6, Pallas kernels: none -> 58.1 us  [the longest x1 41.2 us: ladder_of(): pl.pallas_call(functools.partial(ladder_kernel, pieces=len(pieces), group...]
    reduce_scatter x1 -> x0, waiting for transfers between devices: 56.4 us -> none  [shards(): lax.psum_scatter(partial_value, 'col', scatter_dimension=2, tiled=True)]
    all_gather x1 -> x0, waiting for transfers between devices: 44.3 us -> none  [shards(): gathered = lax.all_gather(window_local, 'col', axis=0, tiled=True)]
    all_to_all x0 -> x1, blocking collectives: none -> 20.9 us  [part(): lax.all_to_all(summed, 'col', 0, 0, tiled=True, axis_index_groups=groups)]
    ppermute x0 -> x16, waiting for transfers between devices: none -> 12.9 us  [the longest x7 11.4 us: hop(): return lax.ppermute(piece, 'col', along(step))]
    ppermute x0 -> x16, starting transfers between devices: none -> 10.6 us  [the longest x7 8.96 us: hop(): return lax.ppermute(piece, 'col', along(step))]
    slice x1 -> x0, local copies, waits for them, and re-layouts: 7.51 us -> none  [shards(): window_local = jnp.transpose(cholesky[:, :, :A_WIN], (0, 2, 1))]
  transfers between devices with their start and end apart: 2 -> 16, of which waited for: 2 -> 6; matrix products, arithmetic and copies ran while one was open for 0% -> 0% of each run, Pallas kernels for 0% -> 12%
where the time goes in v1:
time: 104 us; the launch traced here: 103 us
  Pallas kernels  58.1 us (56%)
  blocking collectives  20.9 us (20%)
  waiting for transfers between devices  12.9 us (12%)
  starting transfers between devices  10.6 us (10%)
    pallas_call x1, Pallas kernels, ladder_of(): pl.pallas_call(functools.partial(ladder_kernel, pieces=len(pieces), group...  41.2 us
    all_to_all x1, blocking collectives, part(): lax.all_to_all(summed, 'col', 0, 0, tiled=True, axis_index_groups=groups)  20.9 us
    pallas_call x4, Pallas kernels, turn(): pl.pallas_call(functools.partial(turn_kernel, first=part * tile), out_sha...  12.2 us
    ppermute x7, waiting for transfers between devices, hop(): return lax.ppermute(piece, 'col', along(step))  11.4 us
    ppermute x7, starting transfers between devices, hop(): return lax.ppermute(piece, 'col', along(step))  8.96 us
    pallas_call x1, Pallas kernels, window_of(): pl.pallas_call(window_kernel, out_shape=jax.ShapeDtypeStruct((A_WIN, own,...  4.67 us
  transfers between devices with their start and end apart: 16, of which 6 were waited for; matrix products, arithmetic and copies ran while one was open for 0% of the time, Pallas kernels for 12%

profile of v1, /device:TPU:0, one launch (start us, length us, event | category | flops | bytes accessed | tf_op | source)
XLA Modules:
  0.0 103.4 jit_solution(17483005517707758851)
XLA Ops:
  0.0 4.7 %window.1.refs_0_ = bf16[2,32,1024]{2,1,0:T(8,128)(2,1)S(1)} custom-call(bf16[32,1024,512]{2,1,0:T(8,128)(2,1)} %refs_17_.1), custom_call_target="tpu_custom_call" | custom-call | bytes 8388608 | tf_op jit(solution)/shard_map/window/pallas_call | solution.py:50
  4.7 3.1 %collective-permute-start = (bf16[2,32,1024]{2,1,0:T(8,128)(2,1)S(1)}, bf16[2,32,1024]{2,1,0:T(8,128)(2,1)S(1)}, u32[]{:S(2)}, u32[]{:S(2)}) collective-permute-start(bf16[2,32,1024]{2,1,0:T(8,128)(2,1)S(1)} %window.1.refs_0_), channel_id=1, source_target_pairs={{0,4},{1,5},{4,8},{5,9},{8,12},{9,13},{12,14},{13,15},{14,10},{15,... | collective-permute-start | bytes 393224 | tf_op jit(solution)/shard_map/ppermute | solution.py:224
  7.8 3.4 %collective-permute-done.refs_1_ = bf16[2,32,1024]{2,1,0:T(8,128)(2,1)S(1)} collective-permute-done((bf16[2,32,1024]{2,1,0:T(8,128)(2,1)S(1)}, bf16[2,32,1024]{2,1,0:T(8,128)(2,1)S(1)}, u32[]{:S(2)}, u32[]{:S(2)}) %collective-permute-start) | collective-permute-done | bytes 131104 | tf_op jit(solution)/shard_map/ppermute | solution.py:224
  11.2 1.8 %collective-permute-start.2 = (bf16[2,32,1024]{2,1,0:T(8,128)(2,1)S(1)}, bf16[2,32,1024]{2,1,0:T(8,128)(2,1)S(1)}, u32[]{:S(2)}, u32[]{:S(2)}) collective-permute-start(bf16[2,32,1024]{2,1,0:T(8,128)(2,1)S(1)} %collective-permute-done.refs_1_), channel_id=1, source_target_pairs={{0,4},{1,5},{4,8},{5,9},{8,12},{9,13},{12,14},{13,15},{14,10},{15,... | collective-permute-start | bytes 393224 | tf_op jit(solution)/shard_map/ppermute | solution.py:224
  13.0 0.2 collective-permute-start.3
  13.3 2.9 %collective-permute-done.2.refs_3_ = bf16[2,32,1024]{2,1,0:T(8,128)(2,1)S(1)} collective-permute-done((bf16[2,32,1024]{2,1,0:T(8,128)(2,1)S(1)}, bf16[2,32,1024]{2,1,0:T(8,128)(2,1)S(1)}, u32[]{:S(2)}, u32[]{:S(2)}) %collective-permute-start.2) | collective-permute-done | bytes 131104 | tf_op jit(solution)/shard_map/ppermute | solution.py:224
  16.2 1.8 %collective-permute-start.4 = (bf16[2,32,1024]{2,1,0:T(8,128)(2,1)S(1)}, bf16[2,32,1024]{2,1,0:T(8,128)(2,1)S(1)}, u32[]{:S(2)}, u32[]{:S(2)}) collective-permute-start(bf16[2,32,1024]{2,1,0:T(8,128)(2,1)S(1)} %collective-permute-done.2.refs_3_), channel_id=1, source_target_pairs={{0,4},{1,5},{4,8},{5,9},{8,12},{9,13},{12,14},{13,15},{14,10},{15,... | collective-permute-start | bytes 393224 | tf_op jit(solution)/shard_map/ppermute | solution.py:224
  18.0 0.5 collective-permute-start.9
  18.5 0.2 collective-permute-start.5
  18.7 2.4 %collective-permute-done.4.refs_5_ = bf16[2,32,1024]{2,1,0:T(8,128)(2,1)S(1)} collective-permute-done((bf16[2,32,1024]{2,1,0:T(8,128)(2,1)S(1)}, bf16[2,32,1024]{2,1,0:T(8,128)(2,1)S(1)}, u32[]{:S(2)}, u32[]{:S(2)}) %collective-permute-start.4) | collective-permute-done | bytes 131104 | tf_op jit(solution)/shard_map/ppermute | solution.py:224
  21.2 1.8 %collective-permute-start.6 = (bf16[2,32,1024]{2,1,0:T(8,128)(2,1)S(1)}, bf16[2,32,1024]{2,1,0:T(8,128)(2,1)S(1)}, u32[]{:S(2)}, u32[]{:S(2)}) collective-permute-start(bf16[2,32,1024]{2,1,0:T(8,128)(2,1)S(1)} %collective-permute-done.4.refs_5_), channel_id=1, source_target_pairs={{0,4},{1,5},{4,8},{5,9},{8,12},{9,13},{12,14},{13,15},{14,10},{15,... | collective-permute-start | bytes 393224 | tf_op jit(solution)/shard_map/ppermute | solution.py:224
  23.0 0.5 collective-permute-start.10
  23.6 0.9 collective-permute-done.5.refs_6_
  24.4 1.7 %collective-permute-done.6.refs_7_ = bf16[2,32,1024]{2,1,0:T(8,128)(2,1)S(1)} collective-permute-done((bf16[2,32,1024]{2,1,0:T(8,128)(2,1)S(1)}, bf16[2,32,1024]{2,1,0:T(8,128)(2,1)S(1)}, u32[]{:S(2)}, u32[]{:S(2)}) %collective-permute-start.6) | collective-permute-done | bytes 131104 | tf_op jit(solution)/shard_map/ppermute | solution.py:224
  26.1 3.1 %turn.4.refs_0_ = bf16[32,256,512]{2,1,0:T(8,128)(2,1)} custom-call(bf16[256,32,512]{2,1,0:T(8,128)(2,1)} %amp_ref.7), custom_call_target="tpu_custom_call" | custom-call | bytes 4194304 | tf_op jit(solution)/shard_map/turn/pallas_call | solution.py:96
  29.2 3.0 %turn.5.refs_0_ = bf16[32,256,512]{2,1,0:T(8,128)(2,1)} custom-call(bf16[256,32,512]{2,1,0:T(8,128)(2,1)} %amp_ref.7, bf16[32,256,512]{2,1,0:T(8,128)(2,1)} %turn.4.refs_0_), custom_call_target="tpu_custom_call", output_to_operand_aliasing={{}: (1, {})} | custom-call | bytes 4194304 | tf_op jit(solution)/shard_map/turn/pallas_call | solution.py:96
  32.2 3.1 %turn.6.refs_0_ = bf16[32,256,512]{2,1,0:T(8,128)(2,1)} custom-call(bf16[256,32,512]{2,1,0:T(8,128)(2,1)} %amp_ref.7, bf16[32,256,512]{2,1,0:T(8,128)(2,1)} %turn.5.refs_0_), custom_call_target="tpu_custom_call", output_to_operand_aliasing={{}: (1, {})} | custom-call | bytes 4194304 | tf_op jit(solution)/shard_map/turn/pallas_call | solution.py:96
  35.3 3.0 %turn.7.refs_16_ = bf16[32,256,512]{2,1,0:T(8,128)(2,1)} custom-call(bf16[256,32,512]{2,1,0:T(8,128)(2,1)} %amp_ref.7, bf16[32,256,512]{2,1,0:T(8,128)(2,1)} %turn.6.refs_0_), custom_call_target="tpu_custom_call", output_to_operand_aliasing={{}: (1, {})} | custom-call | bytes 4194304 | tf_op jit(solution)/shard_map/turn/pallas_call | solution.py:96
  38.3 0.1 stack.71.order_ref
  38.5 41.2 %ladder.1 = (f32[8,2,32,256]{3,2,1,0:T(8,128)S(1)}, f32[8,2,32,256]{3,2,1,0:T(8,128)S(1)}) custom-call(s32[17]{0:T(128)S(1)} %stack.71.order_ref, bf16[2,32,1024]{2,1,0:T(8,128)(2,1)S(1)} %window.1.refs_0_, bf16[2,32,1024]{2,1,0:T(8,128)(2,1)S(1)} %collective-permute-done.refs_1_, bf16[2,32,1024]{2,1,0:T(8,128)(2,1)S(1)} %collective-permute-done.1.refs_2_, ...), custom_call_target="tpu_custom_call" | custom-call | flops 34359738368 | bytes 41943040 | tf_op jit(solution)/shard_map/ladder/pallas_call | solution.py:179
  79.7 0.6 collective-permute-start.15
  80.3 1.5 %collective-permute-done.15 = f32[8,2,32,256]{3,2,1,0:T(8,128)S(1)} collective-permute-done((f32[8,2,32,256]{3,2,1,0:T(8,128)S(1)}, f32[8,2,32,256]{3,2,1,0:T(8,128)S(1)}, u32[]{:S(2)}, u32[]{:S(2)}) %collective-permute-start.15) | collective-permute-done | bytes 524320 | tf_op jit(solution)/shard_map/ppermute | solution.py:252
  81.9 20.9 %all_to_all.5 = f32[8,2,32,256]{3,2,1,0:T(8,128)S(1)} all-to-all(f32[8,2,32,256]{3,2,1,0:T(8,128)S(1)} %add.430), channel_id=1, replica_groups={{0,2,4,6,8,10,12,14},{1,3,5,7,9,11,13,15},{16,18,20,22,24,26,28,30},{17..., dimensions={0} | all-to-all | bytes 1048576 | tf_op jit(solution)/shard_map/all_to_all | solution.py:254
  102.8 0.7 reduce_sum.9
  (18 shorter events, 0.2 us)
Async XLA Ops:
  4.7 6.5 %collective-permute-start = (bf16[2,32,1024]{2,1,0:T(8,128)(2,1)S(1)}, bf16[2,32,1024]{2,1,0:T(8,128)(2,1)S(1)}, u32[]{:S(2)}, u32[]{:S(2)}) collective-permute-start(bf16[2,32,1024]{2,1,0:T(8,128)(2,1)S(1)} %window.1.refs_0_), channel_id=1, source_target_pairs={{0,4},{1,5},{4,8},{5,9},{8,12},{9,13},{12,14},{13,15},{14,10},{15,... | collective-permute-start | bytes 393224 | tf_op jit(solution)/shard_map/ppermute | solution.py:224
  7.8 5.2 %collective-permute-start.1 = (bf16[2,32,1024]{2,1,0:T(8,128)(2,1)S(1)}, bf16[2,32,1024]{2,1,0:T(8,128)(2,1)S(1)}, u32[]{:S(2)}, u32[]{:S(2)}) collective-permute-start(bf16[2,32,1024]{2,1,0:T(8,128)(2,1)S(1)} %window.1.refs_0_), channel_id=1, source_target_pairs={{0,2},{1,3},{4,0},{5,1},{8,4},{9,5},{12,8},{13,9},{14,12},{15,13},... | collective-permute-start | bytes 393224 | tf_op jit(solution)/shard_map/ppermute | solution.py:224
  11.2 5.0 %collective-permute-start.2 = (bf16[2,32,1024]{2,1,0:T(8,128)(2,1)S(1)}, bf16[2,32,1024]{2,1,0:T(8,128)(2,1)S(1)}, u32[]{:S(2)}, u32[]{:S(2)}) collective-permute-start(bf16[2,32,1024]{2,1,0:T(8,128)(2,1)S(1)} %collective-permute-done.refs_1_), channel_id=1, source_target_pairs={{0,4},{1,5},{4,8},{5,9},{8,12},{9,13},{12,14},{13,15},{14,10},{15,... | collective-permute-start | bytes 393224 | tf_op jit(solution)/shard_map/ppermute | solution.py:224
  13.0 5.5 %collective-permute-start.3 = (bf16[2,32,1024]{2,1,0:T(8,128)(2,1)S(1)}, bf16[2,32,1024]{2,1,0:T(8,128)(2,1)S(1)}, u32[]{:S(2)}, u32[]{:S(2)}) collective-permute-start(bf16[2,32,1024]{2,1,0:T(8,128)(2,1)S(1)} %collective-permute-done.1.refs_2_), channel_id=1, source_target_pairs={{0,2},{1,3},{4,0},{5,1},{8,4},{9,5},{12,8},{13,9},{14,12},{15,13},... | collective-permute-start | bytes 393224 | tf_op jit(solution)/shard_map/ppermute | solution.py:224
  16.2 5.0 %collective-permute-start.4 = (bf16[2,32,1024]{2,1,0:T(8,128)(2,1)S(1)}, bf16[2,32,1024]{2,1,0:T(8,128)(2,1)S(1)}, u32[]{:S(2)}, u32[]{:S(2)}) collective-permute-start(bf16[2,32,1024]{2,1,0:T(8,128)(2,1)S(1)} %collective-permute-done.2.refs_3_), channel_id=1, source_target_pairs={{0,4},{1,5},{4,8},{5,9},{8,12},{9,13},{12,14},{13,15},{14,10},{15,... | collective-permute-start | bytes 393224 | tf_op jit(solution)/shard_map/ppermute | solution.py:224
  18.0 5.0 %collective-permute-start.7 = (bf16[2,32,1024]{2,1,0:T(8,128)(2,1)S(1)}, bf16[2,32,1024]{2,1,0:T(8,128)(2,1)S(1)}, u32[]{:S(2)}, u32[]{:S(2)}) collective-permute-start(bf16[2,32,1024]{2,1,0:T(8,128)(2,1)S(1)} %window.1.refs_0_), channel_id=1, source_target_pairs={{0,1},{1,0},{2,3},{3,2},{4,5},{5,4},{6,7},{7,6},{8,9},{9,8},{10,11... | collective-permute-start | bytes 393224 | tf_op jit(solution)/shard_map/ppermute | solution.py:237
  18.0 5.0 %collective-permute-start.9 = (bf16[2,32,1024]{2,1,0:T(8,128)(2,1)S(1)}, bf16[2,32,1024]{2,1,0:T(8,128)(2,1)S(1)}, u32[]{:S(2)}, u32[]{:S(2)}) collective-permute-start(bf16[2,32,1024]{2,1,0:T(8,128)(2,1)S(1)} %collective-permute-done.1.refs_2_), channel_id=1, source_target_pairs={{0,1},{1,0},{2,3},{3,2},{4,5},{5,4},{6,7},{7,6},{8,9},{9,8},{10,11... | collective-permute-start | bytes 393224 | tf_op jit(solution)/shard_map/ppermute | solution.py:237
  18.5 5.0 %collective-permute-start.8 = (bf16[2,32,1024]{2,1,0:T(8,128)(2,1)S(1)}, bf16[2,32,1024]{2,1,0:T(8,128)(2,1)S(1)}, u32[]{:S(2)}, u32[]{:S(2)}) collective-permute-start(bf16[2,32,1024]{2,1,0:T(8,128)(2,1)S(1)} %collective-permute-done.refs_1_), channel_id=1, source_target_pairs={{0,1},{1,0},{2,3},{3,2},{4,5},{5,4},{6,7},{7,6},{8,9},{9,8},{10,11... | collective-permute-start | bytes 393224 | tf_op jit(solution)/shard_map/ppermute | solution.py:237
  18.5 5.9 %collective-permute-start.5 = (bf16[2,32,1024]{2,1,0:T(8,128)(2,1)S(1)}, bf16[2,32,1024]{2,1,0:T(8,128)(2,1)S(1)}, u32[]{:S(2)}, u32[]{:S(2)}) collective-permute-start(bf16[2,32,1024]{2,1,0:T(8,128)(2,1)S(1)} %collective-permute-done.3.refs_4_), channel_id=1, source_target_pairs={{0,2},{1,3},{4,0},{5,1},{8,4},{9,5},{12,8},{13,9},{14,12},{15,13},... | collective-permute-start | bytes 393224 | tf_op jit(solution)/shard_map/ppermute | solution.py:224
  21.2 5.0 %collective-permute-start.6 = (bf16[2,32,1024]{2,1,0:T(8,128)(2,1)S(1)}, bf16[2,32,1024]{2,1,0:T(8,128)(2,1)S(1)}, u32[]{:S(2)}, u32[]{:S(2)}) collective-permute-start(bf16[2,32,1024]{2,1,0:T(8,128)(2,1)S(1)} %collective-permute-done.4.refs_5_), channel_id=1, source_target_pairs={{0,4},{1,5},{4,8},{5,9},{8,12},{9,13},{12,14},{13,15},{14,10},{15,... | collective-permute-start | bytes 393224 | tf_op jit(solution)/shard_map/ppermute | solution.py:224
  23.0 15.5 %collective-permute-start.11 = (bf16[2,32,1024]{2,1,0:T(8,128)(2,1)S(1)}, bf16[2,32,1024]{2,1,0:T(8,128)(2,1)S(1)}, u32[]{:S(2)}, u32[]{:S(2)}) collective-permute-start(bf16[2,32,1024]{2,1,0:T(8,128)(2,1)S(1)} %collective-permute-done.3.refs_4_), channel_id=1, source_target_pairs={{0,1},{1,0},{2,3},{3,2},{4,5},{5,4},{6,7},{7,6},{8,9},{9,8},{10,11... | collective-permute-start | bytes 393224 | tf_op jit(solution)/shard_map/ppermute | solution.py:237
  23.0 15.5 %collective-permute-start.10 = (bf16[2,32,1024]{2,1,0:T(8,128)(2,1)S(1)}, bf16[2,32,1024]{2,1,0:T(8,128)(2,1)S(1)}, u32[]{:S(2)}, u32[]{:S(2)}) collective-permute-start(bf16[2,32,1024]{2,1,0:T(8,128)(2,1)S(1)} %collective-permute-done.2.refs_3_), channel_id=1, source_target_pairs={{0,1},{1,0},{2,3},{3,2},{4,5},{5,4},{6,7},{7,6},{8,9},{9,8},{10,11... | collective-permute-start | bytes 393224 | tf_op jit(solution)/shard_map/ppermute | solution.py:237
  23.5 15.0 %collective-permute-start.12 = (bf16[2,32,1024]{2,1,0:T(8,128)(2,1)S(1)}, bf16[2,32,1024]{2,1,0:T(8,128)(2,1)S(1)}, u32[]{:S(2)}, u32[]{:S(2)}) collective-permute-start(bf16[2,32,1024]{2,1,0:T(8,128)(2,1)S(1)} %collective-permute-done.4.refs_5_), channel_id=1, source_target_pairs={{0,1},{1,0},{2,3},{3,2},{4,5},{5,4},{6,7},{7,6},{8,9},{9,8},{10,11... | collective-permute-start | bytes 393224 | tf_op jit(solution)/shard_map/ppermute | solution.py:237
  24.4 14.0 %collective-permute-start.13 = (bf16[2,32,1024]{2,1,0:T(8,128)(2,1)S(1)}, bf16[2,32,1024]{2,1,0:T(8,128)(2,1)S(1)}, u32[]{:S(2)}, u32[]{:S(2)}) collective-permute-start(bf16[2,32,1024]{2,1,0:T(8,128)(2,1)S(1)} %collective-permute-done.5.refs_6_), channel_id=1, source_target_pairs={{0,1},{1,0},{2,3},{3,2},{4,5},{5,4},{6,7},{7,6},{8,9},{9,8},{10,11... | collective-permute-start | bytes 393224 | tf_op jit(solution)/shard_map/ppermute | solution.py:237
  26.1 12.4 %collective-permute-start.14 = (bf16[2,32,1024]{2,1,0:T(8,128)(2,1)S(1)}, bf16[2,32,1024]{2,1,0:T(8,128)(2,1)S(1)}, u32[]{:S(2)}, u32[]{:S(2)}) collective-permute-start(bf16[2,32,1024]{2,1,0:T(8,128)(2,1)S(1)} %collective-permute-done.6.refs_7_), channel_id=1, source_target_pairs={{0,1},{1,0},{2,3},{3,2},{4,5},{5,4},{6,7},{7,6},{8,9},{9,8},{10,11... | collective-permute-start | bytes 393224 | tf_op jit(solution)/shard_map/ppermute | solution.py:237
  79.7 2.1 %collective-permute-start.15 = (f32[8,2,32,256]{3,2,1,0:T(8,128)S(1)}, f32[8,2,32,256]{3,2,1,0:T(8,128)S(1)}, u32[]{:S(2)}, u32[]{:S(2)}) collective-permute-start(f32[8,2,32,256]{3,2,1,0:T(8,128)S(1)} %get-tuple-element.8), channel_id=1, source_target_pairs={{0,1},{1,0},{2,3},{3,2},{4,5},{5,4},{6,7},{7,6},{8,9},{9,8},{10,11... | collective-permute-start | bytes 1572872 | tf_op jit(solution)/shard_map/ppermute | solution.py:252

commit v2 on v1

--- a/solution.py
+++ b/solution.py
@@ -12,7 +12,8 @@
 CORES = 2
 LANES = 128
 MIB = 1 << 20
-GROUP = 8
+GROUP = 32
+SLOTS = 4
 GRANT = 48 * MIB
 
 
@@ -88,7 +89,7 @@
 def turn(amplitudes, part, parts, held):
     pairs, steps, orbitals = amplitudes.shape
     tile = max(steps // parts, min(8, steps))
-    rows = min(64, pairs)
+    rows = min(32, pairs)
     chunks = pairs // rows
     if part * tile >= steps:
         return held
@@ -112,49 +113,48 @@
     )(amplitudes, *extra)
 
 
-def ladder_kernel(order_ref, *refs, pieces, group):
+def ladder_kernel(order_ref, *refs, pieces, group, slots):
     piece_refs = refs[:pieces]
-    amp_ref, chol_ref, keep_ref, send_ref, window, amps, chols, half, total, came, amp_came, chol_came = refs[pieces:]
+    amp_ref, chol_ref, keep_ref, send_ref, window, amps, chols, half, total, amp_came, chol_came = refs[pieces:]
     own = piece_refs[0].shape[1]
     steps, pairs, _ = amp_ref.shape
     groups = steps // group
 
-    def fetch(g, slot, c):
-        at = g * group + c
+    def fetch(at, slot):
         return (
-            pltpu.make_async_copy(amp_ref.at[at], amps.at[slot, c], amp_came.at[slot, c]),
-            pltpu.make_async_copy(chol_ref.at[at], chols.at[slot, c], chol_came.at[slot, c]),
+            pltpu.make_async_copy(amp_ref.at[at], amps.at[slot], amp_came.at[slot]),
+            pltpu.make_async_copy(chol_ref.at[at], chols.at[slot], chol_came.at[slot]),
         )
 
-    gathered = []
+    for c in range(2):
+        for copy in fetch(c, c):
+            copy.start()
+    for c in range(2, slots - 1):
+        for copy in fetch(c, c):
+            copy.start()
+    total[...] = jnp.zeros_like(total)
     for i in range(pieces):
         start = pl.multiple_of(order_ref[i] * own, own)
-        gathered.append(pltpu.make_async_copy(piece_refs[i], window.at[:, pl.ds(start, own), :], came.at[i]))
-        gathered[i].start()
-    for c in range(group):
-        for copy in fetch(0, 0, c):
-            copy.start()
-    total[...] = jnp.zeros_like(total)
-    for copy in gathered:
-        copy.wait()
+        for a in range(A_WIN):
+            window[a, pl.ds(start, own), :] = piece_refs[i][a]
 
     def advance(g, _):
-        slot = lax.rem(g, 2)
-
-        @pl.when(g + 1 < groups)
-        def _():
-            for c in range(group):
-                for copy in fetch(g + 1, 1 - slot, c):
+        for u in range(group):
+            at = g * group + u
+            slot, spare = u % slots, (u - 1) % slots
+            for copy in fetch(at, slot):
+                copy.wait()
+
+            @pl.when(at + slots - 1 < steps)
+            def _():
+                for copy in fetch(at + slots - 1, spare):
                     copy.start()
 
-        for c in range(group):
-            for copy in fetch(g, slot, c):
-                copy.wait()
             for a in range(A_WIN):
-                half[c, a * pairs : (a + 1) * pairs, :] = jnp.dot(
-                    amps[slot, c], window[a], preferred_element_type=jnp.float32
+                half[u % 2, a * pairs : (a + 1) * pairs, :] = jnp.dot(
+                    amps[slot], window[a], preferred_element_type=jnp.float32
                 ).astype(half.dtype)
-            total[...] += jnp.dot(half[c], chols[slot, c], preferred_element_type=jnp.float32)
+            total[...] += jnp.dot(half[u % 2], chols[slot], preferred_element_type=jnp.float32)
         return 0
 
     lax.fori_loop(0, groups, advance, 0)
@@ -172,26 +172,26 @@
     steps, pairs, orbitals = amplitudes.shape
     _, depth, _ = cholesky.shape
     group = GROUP if steps % GROUP == 0 else 1
+    slots = min(SLOTS, group)
     width = orbitals // (chips * CORES)
     shape = jax.ShapeDtypeStruct((chips, A_WIN, width, pairs), jnp.float32)
     flops = 2 * steps * pairs * A_WIN * orbitals * depth * 2
     kind = amplitudes.dtype
     return pl.pallas_call(
-        functools.partial(ladder_kernel, pieces=len(pieces), group=group),
+        functools.partial(ladder_kernel, pieces=len(pieces), group=group, slots=slots),
         out_shape=(shape, shape),
         in_specs=[pl.BlockSpec(memory_space=pltpu.SMEM)]
-        + [pl.BlockSpec(memory_space=pl.ANY)] * len(pieces)
+        + [pl.BlockSpec(memory_space=pltpu.VMEM)] * len(pieces)
         + [pl.BlockSpec(memory_space=pltpu.HBM)] * 2,
         out_specs=[pl.BlockSpec(memory_space=pltpu.VMEM)] * 2,
         scratch_shapes=[
             pltpu.VMEM((A_WIN, orbitals, depth), kind),
-            pltpu.VMEM((2, group, pairs, orbitals), kind),
-            pltpu.VMEM((2, group, depth, orbitals), kind),
-            pltpu.VMEM((group, A_WIN * pairs, depth), kind),
+            pltpu.VMEM((slots, pairs, orbitals), kind),
+            pltpu.VMEM((slots, depth, orbitals), kind),
+            pltpu.VMEM((2, A_WIN * pairs, depth), kind),
             pltpu.VMEM((A_WIN * pairs, orbitals), jnp.float32),
-            pltpu.SemaphoreType.DMA((len(pieces),)),
-            pltpu.SemaphoreType.DMA((2, group)),
-            pltpu.SemaphoreType.DMA((2, group)),
+            pltpu.SemaphoreType.DMA((slots,)),
+            pltpu.SemaphoreType.DMA((slots,)),
         ],
         cost_estimate=pl.CostEstimate(
             flops=flops, bytes_accessed=2 * (cholesky.size + amplitudes.size), transcendentals=0
@@ -251,8 +251,10 @@
     keep, send = ladder_of(order, pieces, by_step, cholesky, chips)
     summed = keep + lax.ppermute(send, "col", partner)
     groups = [[chip * CORES + c for chip in range(chips)] for c in range(CORES)]
-    parts = lax.all_to_all(summed, "col", 0, 0, tiled=True, axis_index_groups=groups)
-    return jnp.transpose(parts.sum(0), (2, 0, 1))
+    parts = lax.all_to_all(summed.astype(jnp.bfloat16), "col", 0, 0, tiled=True, axis_index_groups=groups)
+    mine_at = lax.broadcasted_iota(jnp.int32, (chips, 1, 1, 1), 0) == me // CORES
+    ladder = jnp.where(mine_at, summed, parts.astype(jnp.float32)).sum(0)
+    return jnp.transpose(ladder, (2, 0, 1))
 
 
 def solution(mesh):

time: 104 us -> 96.3 us (0.926)
  blocking collectives: 20.9 us -> 0 us
  waiting for transfers between devices: 12.9 us -> 22.4 us
  starting transfers between devices: 10.6 us -> 16.7 us
  Pallas kernels: 58.1 us -> 55.2 us
    all_to_all x1 -> x0, blocking collectives: 20.9 us -> none  [part(): lax.all_to_all(summed, 'col', 0, 0, tiled=True, axis_index_groups=groups)]
    all_to_all x0 -> x1, waiting for transfers between devices: none -> 9.45 us  [part(): lax.all_to_all(summed.astype(jnp.bfloat16), 'col', 0, 0, tiled=True, axis...]
    all_to_all x0 -> x1, starting transfers between devices: none -> 6.05 us  [part(): lax.all_to_all(summed.astype(jnp.bfloat16), 'col', 0, 0, tiled=True, axis...]
    pallas_call x1, Pallas kernels: 41.2 us -> 39.2 us  [ladder_of(): pl.pallas_call(functools.partial(ladder_kernel, pieces=len(pieces), group...]
  transfers between devices with their start and end apart: 16 -> 17, of which waited for: 6 -> 7; matrix products, arithmetic and copies ran while one was open for 0% -> 0% of each run, Pallas kernels for 12% -> 12%
where the time goes in v2:
time: 96.3 us; the launch traced here: 96 us
  Pallas kernels  55.2 us (57%)
  waiting for transfers between devices  22.4 us (23%)
  starting transfers between devices  16.7 us (17%)
  other arithmetic  1.54 us (2%)
    pallas_call x1, Pallas kernels, ladder_of(): pl.pallas_call(functools.partial(ladder_kernel, pieces=len(pieces), group...  39.2 us
    ppermute x7, waiting for transfers between devices, hop(): return lax.ppermute(piece, 'col', along(step))  11.4 us
    pallas_call x4, Pallas kernels, turn(): pl.pallas_call(functools.partial(turn_kernel, first=part * tile), out_sha...  11.3 us
    all_to_all x1, waiting for transfers between devices, part(): lax.all_to_all(summed.astype(jnp.bfloat16), 'col', 0, 0, tiled=True, axis...  9.45 us
    ppermute x7, starting transfers between devices, hop(): return lax.ppermute(piece, 'col', along(step))  8.96 us
    all_to_all x1, starting transfers between devices, part(): lax.all_to_all(summed.astype(jnp.bfloat16), 'col', 0, 0, tiled=True, axis...  6.05 us
    pallas_call x1, Pallas kernels, window_of(): pl.pallas_call(window_kernel, out_shape=jax.ShapeDtypeStruct((A_WIN, own,...  4.67 us
  transfers between devices with their start and end apart: 17, of which 7 were waited for; matrix products, arithmetic and copies ran while one was open for 0% of the time, Pallas kernels for 12%

profile of v2, /device:TPU:0, one launch (start us, length us, event | category | flops | bytes accessed | tf_op | source)
XLA Modules:
  0.0 96.0 jit_solution(9993052317912701925)
XLA Ops:
  0.0 4.7 %window.1.refs_0_ = bf16[2,32,1024]{2,1,0:T(8,128)(2,1)S(1)} custom-call(bf16[32,1024,512]{2,1,0:T(8,128)(2,1)} %refs_17_.1), custom_call_target="tpu_custom_call" | custom-call | bytes 8388608 | tf_op jit(solution)/shard_map/window/pallas_call | solution.py:51
  4.7 3.1 %collective-permute-start = (bf16[2,32,1024]{2,1,0:T(8,128)(2,1)S(1)}, bf16[2,32,1024]{2,1,0:T(8,128)(2,1)S(1)}, u32[]{:S(2)}, u32[]{:S(2)}) collective-permute-start(bf16[2,32,1024]{2,1,0:T(8,128)(2,1)S(1)} %window.1.refs_0_), channel_id=1, source_target_pairs={{0,4},{1,5},{4,8},{5,9},{8,12},{9,13},{12,14},{13,15},{14,10},{15,... | collective-permute-start | bytes 393224 | tf_op jit(solution)/shard_map/ppermute | solution.py:224
  7.8 3.4 %collective-permute-done.refs_1_ = bf16[2,32,1024]{2,1,0:T(8,128)(2,1)S(1)} collective-permute-done((bf16[2,32,1024]{2,1,0:T(8,128)(2,1)S(1)}, bf16[2,32,1024]{2,1,0:T(8,128)(2,1)S(1)}, u32[]{:S(2)}, u32[]{:S(2)}) %collective-permute-start) | collective-permute-done | bytes 131104 | tf_op jit(solution)/shard_map/ppermute | solution.py:224
  11.2 1.8 %collective-permute-start.2 = (bf16[2,32,1024]{2,1,0:T(8,128)(2,1)S(1)}, bf16[2,32,1024]{2,1,0:T(8,128)(2,1)S(1)}, u32[]{:S(2)}, u32[]{:S(2)}) collective-permute-start(bf16[2,32,1024]{2,1,0:T(8,128)(2,1)S(1)} %collective-permute-done.refs_1_), channel_id=1, source_target_pairs={{0,4},{1,5},{4,8},{5,9},{8,12},{9,13},{12,14},{13,15},{14,10},{15,... | collective-permute-start | bytes 393224 | tf_op jit(solution)/shard_map/ppermute | solution.py:224
  13.3 2.9 %collective-permute-done.2.refs_3_ = bf16[2,32,1024]{2,1,0:T(8,128)(2,1)S(1)} collective-permute-done((bf16[2,32,1024]{2,1,0:T(8,128)(2,1)S(1)}, bf16[2,32,1024]{2,1,0:T(8,128)(2,1)S(1)}, u32[]{:S(2)}, u32[]{:S(2)}) %collective-permute-start.2) | collective-permute-done | bytes 131104 | tf_op jit(solution)/shard_map/ppermute | solution.py:224
  16.2 1.8 %collective-permute-start.4 = (bf16[2,32,1024]{2,1,0:T(8,128)(2,1)S(1)}, bf16[2,32,1024]{2,1,0:T(8,128)(2,1)S(1)}, u32[]{:S(2)}, u32[]{:S(2)}) collective-permute-start(bf16[2,32,1024]{2,1,0:T(8,128)(2,1)S(1)} %collective-permute-done.2.refs_3_), channel_id=1, source_target_pairs={{0,4},{1,5},{4,8},{5,9},{8,12},{9,13},{12,14},{13,15},{14,10},{15,... | collective-permute-start | bytes 393224 | tf_op jit(solution)/shard_map/ppermute | solution.py:224
  18.0 0.5 collective-permute-start.9
  18.5 0.2 collective-permute-start.5
  18.7 2.4 %collective-permute-done.4.refs_5_ = bf16[2,32,1024]{2,1,0:T(8,128)(2,1)S(1)} collective-permute-done((bf16[2,32,1024]{2,1,0:T(8,128)(2,1)S(1)}, bf16[2,32,1024]{2,1,0:T(8,128)(2,1)S(1)}, u32[]{:S(2)}, u32[]{:S(2)}) %collective-permute-start.4) | collective-permute-done | bytes 131104 | tf_op jit(solution)/shard_map/ppermute | solution.py:224
  21.2 1.8 %collective-permute-start.6 = (bf16[2,32,1024]{2,1,0:T(8,128)(2,1)S(1)}, bf16[2,32,1024]{2,1,0:T(8,128)(2,1)S(1)}, u32[]{:S(2)}, u32[]{:S(2)}) collective-permute-start(bf16[2,32,1024]{2,1,0:T(8,128)(2,1)S(1)} %collective-permute-done.4.refs_5_), channel_id=1, source_target_pairs={{0,4},{1,5},{4,8},{5,9},{8,12},{9,13},{12,14},{13,15},{14,10},{15,... | collective-permute-start | bytes 393224 | tf_op jit(solution)/shard_map/ppermute | solution.py:224
  23.0 0.5 collective-permute-start.10
  23.6 0.9 collective-permute-done.5.refs_6_
  24.4 1.7 %collective-permute-done.6.refs_7_ = bf16[2,32,1024]{2,1,0:T(8,128)(2,1)S(1)} collective-permute-done((bf16[2,32,1024]{2,1,0:T(8,128)(2,1)S(1)}, bf16[2,32,1024]{2,1,0:T(8,128)(2,1)S(1)}, u32[]{:S(2)}, u32[]{:S(2)}) %collective-permute-start.6) | collective-permute-done | bytes 131104 | tf_op jit(solution)/shard_map/ppermute | solution.py:224
  26.1 2.8 %turn.4.refs_0_ = bf16[32,256,512]{2,1,0:T(8,128)(2,1)} custom-call(bf16[256,32,512]{2,1,0:T(8,128)(2,1)} %amp_ref.7), custom_call_target="tpu_custom_call" | custom-call | bytes 4194304 | tf_op jit(solution)/shard_map/turn/pallas_call | solution.py:97
  29.0 2.8 %turn.5.refs_0_ = bf16[32,256,512]{2,1,0:T(8,128)(2,1)} custom-call(bf16[256,32,512]{2,1,0:T(8,128)(2,1)} %amp_ref.7, bf16[32,256,512]{2,1,0:T(8,128)(2,1)} %turn.4.refs_0_), custom_call_target="tpu_custom_call", output_to_operand_aliasing={{}: (1, {})} | custom-call | bytes 4194304 | tf_op jit(solution)/shard_map/turn/pallas_call | solution.py:97
  31.8 2.8 %turn.6.refs_0_ = bf16[32,256,512]{2,1,0:T(8,128)(2,1)} custom-call(bf16[256,32,512]{2,1,0:T(8,128)(2,1)} %amp_ref.7, bf16[32,256,512]{2,1,0:T(8,128)(2,1)} %turn.5.refs_0_), custom_call_target="tpu_custom_call", output_to_operand_aliasing={{}: (1, {})} | custom-call | bytes 4194304 | tf_op jit(solution)/shard_map/turn/pallas_call | solution.py:97
  34.6 2.8 %turn.7.refs_16_ = bf16[32,256,512]{2,1,0:T(8,128)(2,1)} custom-call(bf16[256,32,512]{2,1,0:T(8,128)(2,1)} %amp_ref.7, bf16[32,256,512]{2,1,0:T(8,128)(2,1)} %turn.6.refs_0_), custom_call_target="tpu_custom_call", output_to_operand_aliasing={{}: (1, {})} | custom-call | bytes 4194304 | tf_op jit(solution)/shard_map/turn/pallas_call | solution.py:97
  37.6 39.2 %ladder.1 = (f32[8,2,32,256]{3,2,1,0:T(8,128)S(1)}, f32[8,2,32,256]{3,2,1,0:T(8,128)S(1)}) custom-call(s32[17]{0:T(128)S(1)} %stack.71.order_ref, bf16[2,32,1024]{2,1,0:T(8,128)(2,1)S(1)} %window.1.refs_0_, bf16[2,32,1024]{2,1,0:T(8,128)(2,1)S(1)} %collective-permute-done.refs_1_, bf16[2,32,1024]{2,1,0:T(8,128)(2,1)S(1)} %collective-permute-done.1.refs_2_, ...), custom_call_target="tpu_custom_call" | custom-call | flops 34359738368 | bytes 41943040 | tf_op jit(solution)/shard_map/ladder/pallas_call | solution.py:180
  76.9 0.6 collective-permute-start.15
  77.4 1.5 %collective-permute-done.15 = f32[8,2,32,256]{3,2,1,0:T(8,128)S(1)} collective-permute-done((f32[8,2,32,256]{3,2,1,0:T(8,128)S(1)}, f32[8,2,32,256]{3,2,1,0:T(8,128)S(1)}, u32[]{:S(2)}, u32[]{:S(2)}) %collective-permute-start.15) | collective-permute-done | bytes 524320 | tf_op jit(solution)/shard_map/ppermute | solution.py:252
  79.0 0.8 fusion
  79.8 6.1 %all-to-all-start = ((bf16[8,2,32,256]{3,2,1,0:T(8,128)(2,1)}), bf16[8,2,32,256]{3,2,1,0:T(8,128)(2,1)S(1)}, u32[]{:S(2)}, u32[]{:S(2)}) async-start(bf16[8,2,32,256]{3,2,1,0:T(8,128)(2,1)} %get-tuple-element.9), calls=%async_computation | async-start | bytes 524288 | tf_op jit(solution)/shard_map/all_to_all | solution.py:254
  85.8 9.4 %all-to-all-done = bf16[8,2,32,256]{3,2,1,0:T(8,128)(2,1)S(1)} async-done(((bf16[8,2,32,256]{3,2,1,0:T(8,128)(2,1)}), bf16[8,2,32,256]{3,2,1,0:T(8,128)(2,1)S(1)}, u32[]{:S(2)}, u32[]{:S(2)}) %all-to-all-start) | async-done | bytes 262176 | tf_op jit(solution)/shard_map/all_to_all | solution.py:254
  95.3 0.7 select_reduce_fusion
  (20 shorter events, 0.5 us)
Async XLA Ops:
  4.7 6.5 %collective-permute-start = (bf16[2,32,1024]{2,1,0:T(8,128)(2,1)S(1)}, bf16[2,32,1024]{2,1,0:T(8,128)(2,1)S(1)}, u32[]{:S(2)}, u32[]{:S(2)}) collective-permute-start(bf16[2,32,1024]{2,1,0:T(8,128)(2,1)S(1)} %window.1.refs_0_), channel_id=1, source_target_pairs={{0,4},{1,5},{4,8},{5,9},{8,12},{9,13},{12,14},{13,15},{14,10},{15,... | collective-permute-start | bytes 393224 | tf_op jit(solution)/shard_map/ppermute | solution.py:224
  7.8 5.2 %collective-permute-start.1 = (bf16[2,32,1024]{2,1,0:T(8,128)(2,1)S(1)}, bf16[2,32,1024]{2,1,0:T(8,128)(2,1)S(1)}, u32[]{:S(2)}, u32[]{:S(2)}) collective-permute-start(bf16[2,32,1024]{2,1,0:T(8,128)(2,1)S(1)} %window.1.refs_0_), channel_id=1, source_target_pairs={{0,2},{1,3},{4,0},{5,1},{8,4},{9,5},{12,8},{13,9},{14,12},{15,13},... | collective-permute-start | bytes 393224 | tf_op jit(solution)/shard_map/ppermute | solution.py:224
  11.2 5.0 %collective-permute-start.2 = (bf16[2,32,1024]{2,1,0:T(8,128)(2,1)S(1)}, bf16[2,32,1024]{2,1,0:T(8,128)(2,1)S(1)}, u32[]{:S(2)}, u32[]{:S(2)}) collective-permute-start(bf16[2,32,1024]{2,1,0:T(8,128)(2,1)S(1)} %collective-permute-done.refs_1_), channel_id=1, source_target_pairs={{0,4},{1,5},{4,8},{5,9},{8,12},{9,13},{12,14},{13,15},{14,10},{15,... | collective-permute-start | bytes 393224 | tf_op jit(solution)/shard_map/ppermute | solution.py:224
  13.0 5.5 %collective-permute-start.3 = (bf16[2,32,1024]{2,1,0:T(8,128)(2,1)S(1)}, bf16[2,32,1024]{2,1,0:T(8,128)(2,1)S(1)}, u32[]{:S(2)}, u32[]{:S(2)}) collective-permute-start(bf16[2,32,1024]{2,1,0:T(8,128)(2,1)S(1)} %collective-permute-done.1.refs_2_), channel_id=1, source_target_pairs={{0,2},{1,3},{4,0},{5,1},{8,4},{9,5},{12,8},{13,9},{14,12},{15,13},... | collective-permute-start | bytes 393224 | tf_op jit(solution)/shard_map/ppermute | solution.py:224
  16.2 5.0 %collective-permute-start.4 = (bf16[2,32,1024]{2,1,0:T(8,128)(2,1)S(1)}, bf16[2,32,1024]{2,1,0:T(8,128)(2,1)S(1)}, u32[]{:S(2)}, u32[]{:S(2)}) collective-permute-start(bf16[2,32,1024]{2,1,0:T(8,128)(2,1)S(1)} %collective-permute-done.2.refs_3_), channel_id=1, source_target_pairs={{0,4},{1,5},{4,8},{5,9},{8,12},{9,13},{12,14},{13,15},{14,10},{15,... | collective-permute-start | bytes 393224 | tf_op jit(solution)/shard_map/ppermute | solution.py:224
  18.0 5.0 %collective-permute-start.7 = (bf16[2,32,1024]{2,1,0:T(8,128)(2,1)S(1)}, bf16[2,32,1024]{2,1,0:T(8,128)(2,1)S(1)}, u32[]{:S(2)}, u32[]{:S(2)}) collective-permute-start(bf16[2,32,1024]{2,1,0:T(8,128)(2,1)S(1)} %window.1.refs_0_), channel_id=1, source_target_pairs={{0,1},{1,0},{2,3},{3,2},{4,5},{5,4},{6,7},{7,6},{8,9},{9,8},{10,11... | collective-permute-start | bytes 393224 | tf_op jit(solution)/shard_map/ppermute | solution.py:237
  18.0 5.0 %collective-permute-start.9 = (bf16[2,32,1024]{2,1,0:T(8,128)(2,1)S(1)}, bf16[2,32,1024]{2,1,0:T(8,128)(2,1)S(1)}, u32[]{:S(2)}, u32[]{:S(2)}) collective-permute-start(bf16[2,32,1024]{2,1,0:T(8,128)(2,1)S(1)} %collective-permute-done.1.refs_2_), channel_id=1, source_target_pairs={{0,1},{1,0},{2,3},{3,2},{4,5},{5,4},{6,7},{7,6},{8,9},{9,8},{10,11... | collective-permute-start | bytes 393224 | tf_op jit(solution)/shard_map/ppermute | solution.py:237
  18.5 5.0 %collective-permute-start.8 = (bf16[2,32,1024]{2,1,0:T(8,128)(2,1)S(1)}, bf16[2,32,1024]{2,1,0:T(8,128)(2,1)S(1)}, u32[]{:S(2)}, u32[]{:S(2)}) collective-permute-start(bf16[2,32,1024]{2,1,0:T(8,128)(2,1)S(1)} %collective-permute-done.refs_1_), channel_id=1, source_target_pairs={{0,1},{1,0},{2,3},{3,2},{4,5},{5,4},{6,7},{7,6},{8,9},{9,8},{10,11... | collective-permute-start | bytes 393224 | tf_op jit(solution)/shard_map/ppermute | solution.py:237
  18.5 5.9 %collective-permute-start.5 = (bf16[2,32,1024]{2,1,0:T(8,128)(2,1)S(1)}, bf16[2,32,1024]{2,1,0:T(8,128)(2,1)S(1)}, u32[]{:S(2)}, u32[]{:S(2)}) collective-permute-start(bf16[2,32,1024]{2,1,0:T(8,128)(2,1)S(1)} %collective-permute-done.3.refs_4_), channel_id=1, source_target_pairs={{0,2},{1,3},{4,0},{5,1},{8,4},{9,5},{12,8},{13,9},{14,12},{15,13},... | collective-permute-start | bytes 393224 | tf_op jit(solution)/shard_map/ppermute | solution.py:224
  21.2 5.0 %collective-permute-start.6 = (bf16[2,32,1024]{2,1,0:T(8,128)(2,1)S(1)}, bf16[2,32,1024]{2,1,0:T(8,128)(2,1)S(1)}, u32[]{:S(2)}, u32[]{:S(2)}) collective-permute-start(bf16[2,32,1024]{2,1,0:T(8,128)(2,1)S(1)} %collective-permute-done.4.refs_5_), channel_id=1, source_target_pairs={{0,4},{1,5},{4,8},{5,9},{8,12},{9,13},{12,14},{13,15},{14,10},{15,... | collective-permute-start | bytes 393224 | tf_op jit(solution)/shard_map/ppermute | solution.py:224
  23.0 14.6 %collective-permute-start.11 = (bf16[2,32,1024]{2,1,0:T(8,128)(2,1)S(1)}, bf16[2,32,1024]{2,1,0:T(8,128)(2,1)S(1)}, u32[]{:S(2)}, u32[]{:S(2)}) collective-permute-start(bf16[2,32,1024]{2,1,0:T(8,128)(2,1)S(1)} %collective-permute-done.3.refs_4_), channel_id=1, source_target_pairs={{0,1},{1,0},{2,3},{3,2},{4,5},{5,4},{6,7},{7,6},{8,9},{9,8},{10,11... | collective-permute-start | bytes 393224 | tf_op jit(solution)/shard_map/ppermute | solution.py:237
  23.0 14.6 %collective-permute-start.10 = (bf16[2,32,1024]{2,1,0:T(8,128)(2,1)S(1)}, bf16[2,32,1024]{2,1,0:T(8,128)(2,1)S(1)}, u32[]{:S(2)}, u32[]{:S(2)}) collective-permute-start(bf16[2,32,1024]{2,1,0:T(8,128)(2,1)S(1)} %collective-permute-done.2.refs_3_), channel_id=1, source_target_pairs={{0,1},{1,0},{2,3},{3,2},{4,5},{5,4},{6,7},{7,6},{8,9},{9,8},{10,11... | collective-permute-start | bytes 393224 | tf_op jit(solution)/shard_map/ppermute | solution.py:237
  23.5 14.1 %collective-permute-start.12 = (bf16[2,32,1024]{2,1,0:T(8,128)(2,1)S(1)}, bf16[2,32,1024]{2,1,0:T(8,128)(2,1)S(1)}, u32[]{:S(2)}, u32[]{:S(2)}) collective-permute-start(bf16[2,32,1024]{2,1,0:T(8,128)(2,1)S(1)} %collective-permute-done.4.refs_5_), channel_id=1, source_target_pairs={{0,1},{1,0},{2,3},{3,2},{4,5},{5,4},{6,7},{7,6},{8,9},{9,8},{10,11... | collective-permute-start | bytes 393224 | tf_op jit(solution)/shard_map/ppermute | solution.py:237
  24.4 13.2 %collective-permute-start.13 = (bf16[2,32,1024]{2,1,0:T(8,128)(2,1)S(1)}, bf16[2,32,1024]{2,1,0:T(8,128)(2,1)S(1)}, u32[]{:S(2)}, u32[]{:S(2)}) collective-permute-start(bf16[2,32,1024]{2,1,0:T(8,128)(2,1)S(1)} %collective-permute-done.5.refs_6_), channel_id=1, source_target_pairs={{0,1},{1,0},{2,3},{3,2},{4,5},{5,4},{6,7},{7,6},{8,9},{9,8},{10,11... | collective-permute-start | bytes 393224 | tf_op jit(solution)/shard_map/ppermute | solution.py:237
  26.1 11.5 %collective-permute-start.14 = (bf16[2,32,1024]{2,1,0:T(8,128)(2,1)S(1)}, bf16[2,32,1024]{2,1,0:T(8,128)(2,1)S(1)}, u32[]{:S(2)}, u32[]{:S(2)}) collective-permute-start(bf16[2,32,1024]{2,1,0:T(8,128)(2,1)S(1)} %collective-permute-done.6.refs_7_), channel_id=1, source_target_pairs={{0,1},{1,0},{2,3},{3,2},{4,5},{5,4},{6,7},{7,6},{8,9},{9,8},{10,11... | collective-permute-start | bytes 393224 | tf_op jit(solution)/shard_map/ppermute | solution.py:237
  76.9 2.1 %collective-permute-start.15 = (f32[8,2,32,256]{3,2,1,0:T(8,128)S(1)}, f32[8,2,32,256]{3,2,1,0:T(8,128)S(1)}, u32[]{:S(2)}, u32[]{:S(2)}) collective-permute-start(f32[8,2,32,256]{3,2,1,0:T(8,128)S(1)} %get-tuple-element.8), channel_id=1, source_target_pairs={{0,1},{1,0},{2,3},{3,2},{4,5},{5,4},{6,7},{7,6},{8,9},{9,8},{10,11... | collective-permute-start | bytes 1572872 | tf_op jit(solution)/shard_map/ppermute | solution.py:252
  79.8 15.5 %all-to-all-start = ((bf16[8,2,32,256]{3,2,1,0:T(8,128)(2,1)}), bf16[8,2,32,256]{3,2,1,0:T(8,128)(2,1)S(1)}, u32[]{:S(2)}, u32[]{:S(2)}) async-start(bf16[8,2,32,256]{3,2,1,0:T(8,128)(2,1)} %get-tuple-element.9), calls=%async_computation | async-start | bytes 524288 | tf_op jit(solution)/shard_map/all_to_all | solution.py:254

commit v3 on v2

--- a/solution.py
+++ b/solution.py
@@ -12,8 +12,8 @@
 CORES = 2
 LANES = 128
 MIB = 1 << 20
-GROUP = 32
-SLOTS = 4
+GROUP = 8
+SLOTS = 16
 GRANT = 48 * MIB
 
 
@@ -33,13 +33,21 @@
         copies[i].start()
     source = lax.broadcasted_iota(jnp.int32, (LANES, LANES), 0)
     target = lax.broadcasted_iota(jnp.int32, (LANES, LANES), 1)
-    for row in range(own):
-        hit = source * own + row == target
-        pick[row * LANES : (row + 1) * LANES, :] = jnp.where(hit & (source < A_WIN), 1.0, 0.0).astype(pick.dtype)
+    upper = own // 2
+    for row in range(upper):
+        low = (source < A_WIN) & (source * own + row == target)
+        high = (source >= A_WIN) & (source < 2 * A_WIN) & ((source - A_WIN) * own + upper + row == target)
+        pick[row * LANES : (row + 1) * LANES, :] = jnp.where(low | high, 1.0, 0.0).astype(pick.dtype)
+    first = lax.broadcasted_iota(jnp.int32, (chunk, LANES), 1) < A_WIN
+
+    def joined(row, here):
+        moved = pltpu.roll(rows[upper + row, here, :].astype(jnp.float32), A_WIN, 1)
+        return jnp.where(first, rows[row, here, :].astype(jnp.float32), moved).astype(pick.dtype)
+
     for i in range(depth // chunk):
         here = slice(i * chunk, (i + 1) * chunk)
         copies[i].wait()
-        wide = jnp.concatenate([rows[row, here, :] for row in range(own)], axis=1)
+        wide = jnp.concatenate([joined(row, here) for row in range(upper)], axis=1)
         picked = jnp.dot(wide, pick[...], preferred_element_type=jnp.float32)
         turned = jnp.transpose(picked)
         for a in range(A_WIN):
@@ -55,7 +63,7 @@
         out_specs=pl.BlockSpec(memory_space=pltpu.VMEM),
         scratch_shapes=[
             pltpu.VMEM((own, depth, LANES), cholesky.dtype),
-            pltpu.VMEM((own * LANES, LANES), cholesky.dtype),
+            pltpu.VMEM((own // 2 * LANES, LANES), cholesky.dtype),
             pltpu.SemaphoreType.DMA((4,)),
         ],
         cost_estimate=pl.CostEstimate(flops=0, bytes_accessed=2 * own * depth * LANES, transcendentals=0),
@@ -78,7 +86,7 @@
         comes[i].wait()
         for at in range(0, orbitals, LANES):
             lanes = at // LANES
-            flat[lanes] = taken[i, :, :, at : at + LANES].astype(jnp.float32).reshape(rows * tile, LANES)
+            flat[lanes, : rows * tile] = taken[i, :, :, at : at + LANES].astype(jnp.float32).reshape(rows * tile, LANES)
             for c in range(tile):
                 given[i, c, :, at : at + LANES] = flat[lanes, pl.ds(c, rows, stride=tile), :].astype(given.dtype)
         goes[i].start()
@@ -102,7 +110,7 @@
         scratch_shapes=[
             pltpu.VMEM((chunks, rows, tile, orbitals), amplitudes.dtype),
             pltpu.VMEM((chunks, tile, rows, orbitals), amplitudes.dtype),
-            pltpu.VMEM((orbitals // LANES, rows * tile, LANES), jnp.float32),
+            pltpu.VMEM((orbitals // LANES, (rows + 1) * tile, LANES), jnp.float32),
             pltpu.SemaphoreType.DMA((chunks,)),
             pltpu.SemaphoreType.DMA((chunks,)),
         ],
@@ -113,12 +121,11 @@
     )(amplitudes, *extra)
 
 
-def ladder_kernel(order_ref, *refs, pieces, group, slots):
+def ladder_kernel(order_ref, *refs, pieces, slots):
     piece_refs = refs[:pieces]
     amp_ref, chol_ref, keep_ref, send_ref, window, amps, chols, half, total, amp_came, chol_came = refs[pieces:]
     own = piece_refs[0].shape[1]
     steps, pairs, _ = amp_ref.shape
-    groups = steps // group
 
     def fetch(at, slot):
         return (
@@ -126,38 +133,35 @@
             pltpu.make_async_copy(chol_ref.at[at], chols.at[slot], chol_came.at[slot]),
         )
 
-    for c in range(2):
-        for copy in fetch(c, c):
-            copy.start()
-    for c in range(2, slots - 1):
-        for copy in fetch(c, c):
-            copy.start()
+    def issue(after, upto):
+        for c in range(after, min(upto, steps)):
+            for copy in fetch(c, c % slots):
+                copy.start()
+        return max(after, min(upto, steps))
+
+    issued = issue(0, slots - 1)
     total[...] = jnp.zeros_like(total)
     for i in range(pieces):
         start = pl.multiple_of(order_ref[i] * own, own)
         for a in range(A_WIN):
             window[a, pl.ds(start, own), :] = piece_refs[i][a]
 
-    def advance(g, _):
-        for u in range(group):
-            at = g * group + u
-            slot, spare = u % slots, (u - 1) % slots
-            for copy in fetch(at, slot):
+    first, size = 0, 1
+    while first < steps:
+        here = range(first, min(first + size, steps))
+        for c in here:
+            for copy in fetch(c, c % slots):
                 copy.wait()
-
-            @pl.when(at + slots - 1 < steps)
-            def _():
-                for copy in fetch(at + slots - 1, spare):
-                    copy.start()
-
+        issued = issue(issued, first + slots)
+        for c in here:
             for a in range(A_WIN):
-                half[u % 2, a * pairs : (a + 1) * pairs, :] = jnp.dot(
-                    amps[slot], window[a], preferred_element_type=jnp.float32
+                half[c % 2, a * pairs : (a + 1) * pairs, :] = jnp.dot(
+                    amps[c % slots], window[a], preferred_element_type=jnp.float32
                 ).astype(half.dtype)
-            total[...] += jnp.dot(half[u % 2], chols[slot], preferred_element_type=jnp.float32)
-        return 0
-
-    lax.fori_loop(0, groups, advance, 0)
+            total[...] += jnp.dot(half[c % 2], chols[c % slots], preferred_element_type=jnp.float32)
+        first += size
+        size = min(GROUP, first)
+
     core = order_ref[pieces]
     chips, _, width, _ = keep_ref.shape
     for a in range(A_WIN):
@@ -171,14 +175,13 @@
 def ladder_of(order, pieces, amplitudes, cholesky, chips):
     steps, pairs, orbitals = amplitudes.shape
     _, depth, _ = cholesky.shape
-    group = GROUP if steps % GROUP == 0 else 1
-    slots = min(SLOTS, group)
+    slots = min(SLOTS, steps)
     width = orbitals // (chips * CORES)
     shape = jax.ShapeDtypeStruct((chips, A_WIN, width, pairs), jnp.float32)
     flops = 2 * steps * pairs * A_WIN * orbitals * depth * 2
     kind = amplitudes.dtype
     return pl.pallas_call(
-        functools.partial(ladder_kernel, pieces=len(pieces), group=group, slots=slots),
+        functools.partial(ladder_kernel, pieces=len(pieces), slots=slots),
         out_shape=(shape, shape),
         in_specs=[pl.BlockSpec(memory_space=pltpu.SMEM)]
         + [pl.BlockSpec(memory_space=pltpu.VMEM)] * len(pieces)

time: 96.3 us -> 94.8 us (0.984)
  Pallas kernels: 55.2 us -> 53.7 us
    pallas_call x1, Pallas kernels: 39.2 us -> 38.2 us  [ladder_of(): pl.pallas_call(functools.partial(ladder_kernel, pieces=len(pieces), slots...]
where the time goes in v3:
time: 94.8 us; the launch traced here: 94.5 us
  Pallas kernels  53.7 us (57%)
  waiting for transfers between devices  22.4 us (24%)
  starting transfers between devices  16.7 us (18%)
  other arithmetic  1.54 us (2%)
    pallas_call x1, Pallas kernels, ladder_of(): pl.pallas_call(functools.partial(ladder_kernel, pieces=len(pieces), slots...  38.2 us
    ppermute x7, waiting for transfers between devices, hop(): return lax.ppermute(piece, 'col', along(step))  11.4 us
    pallas_call x4, Pallas kernels, turn(): pl.pallas_call(functools.partial(turn_kernel, first=part * tile), out_sha...  11.3 us
    all_to_all x1, waiting for transfers between devices, part(): lax.all_to_all(summed.astype(jnp.bfloat16), 'col', 0, 0, tiled=True, axis...  9.45 us
    ppermute x7, starting transfers between devices, hop(): return lax.ppermute(piece, 'col', along(step))  8.96 us
    all_to_all x1, starting transfers between devices, part(): lax.all_to_all(summed.astype(jnp.bfloat16), 'col', 0, 0, tiled=True, axis...  6.05 us
    pallas_call x1, Pallas kernels, window_of(): pl.pallas_call(window_kernel, out_shape=jax.ShapeDtypeStruct((A_WIN, own,...  4.24 us
  transfers between devices with their start and end apart: 17, of which 7 were waited for; matrix products, arithmetic and copies ran while one was open for 0% of the time, Pallas kernels for 12%

profile of v3, /device:TPU:0, one launch (start us, length us, event | category | flops | bytes accessed | tf_op | source)
XLA Modules:
  0.0 94.5 jit_solution(7362729980029814438)
XLA Ops:
  0.0 4.2 %window.1.refs_0_ = bf16[2,32,1024]{2,1,0:T(8,128)(2,1)S(1)} custom-call(bf16[32,1024,512]{2,1,0:T(8,128)(2,1)} %refs_17_.1), custom_call_target="tpu_custom_call" | custom-call | bytes 8388608 | tf_op jit(solution)/shard_map/window/pallas_call | solution.py:59
  4.3 3.1 %collective-permute-start = (bf16[2,32,1024]{2,1,0:T(8,128)(2,1)S(1)}, bf16[2,32,1024]{2,1,0:T(8,128)(2,1)S(1)}, u32[]{:S(2)}, u32[]{:S(2)}) collective-permute-start(bf16[2,32,1024]{2,1,0:T(8,128)(2,1)S(1)} %window.1.refs_0_), channel_id=1, source_target_pairs={{0,4},{1,5},{4,8},{5,9},{8,12},{9,13},{12,14},{13,15},{14,10},{15,... | collective-permute-start | bytes 393224 | tf_op jit(solution)/shard_map/ppermute | solution.py:227
  7.4 3.4 %collective-permute-done.refs_1_ = bf16[2,32,1024]{2,1,0:T(8,128)(2,1)S(1)} collective-permute-done((bf16[2,32,1024]{2,1,0:T(8,128)(2,1)S(1)}, bf16[2,32,1024]{2,1,0:T(8,128)(2,1)S(1)}, u32[]{:S(2)}, u32[]{:S(2)}) %collective-permute-start) | collective-permute-done | bytes 131104 | tf_op jit(solution)/shard_map/ppermute | solution.py:227
  10.8 1.8 %collective-permute-start.2 = (bf16[2,32,1024]{2,1,0:T(8,128)(2,1)S(1)}, bf16[2,32,1024]{2,1,0:T(8,128)(2,1)S(1)}, u32[]{:S(2)}, u32[]{:S(2)}) collective-permute-start(bf16[2,32,1024]{2,1,0:T(8,128)(2,1)S(1)} %collective-permute-done.refs_1_), channel_id=1, source_target_pairs={{0,4},{1,5},{4,8},{5,9},{8,12},{9,13},{12,14},{13,15},{14,10},{15,... | collective-permute-start | bytes 393224 | tf_op jit(solution)/shard_map/ppermute | solution.py:227
  12.8 2.9 %collective-permute-done.2.refs_3_ = bf16[2,32,1024]{2,1,0:T(8,128)(2,1)S(1)} collective-permute-done((bf16[2,32,1024]{2,1,0:T(8,128)(2,1)S(1)}, bf16[2,32,1024]{2,1,0:T(8,128)(2,1)S(1)}, u32[]{:S(2)}, u32[]{:S(2)}) %collective-permute-start.2) | collective-permute-done | bytes 131104 | tf_op jit(solution)/shard_map/ppermute | solution.py:227
  15.8 1.8 %collective-permute-start.4 = (bf16[2,32,1024]{2,1,0:T(8,128)(2,1)S(1)}, bf16[2,32,1024]{2,1,0:T(8,128)(2,1)S(1)}, u32[]{:S(2)}, u32[]{:S(2)}) collective-permute-start(bf16[2,32,1024]{2,1,0:T(8,128)(2,1)S(1)} %collective-permute-done.2.refs_3_), channel_id=1, source_target_pairs={{0,4},{1,5},{4,8},{5,9},{8,12},{9,13},{12,14},{13,15},{14,10},{15,... | collective-permute-start | bytes 393224 | tf_op jit(solution)/shard_map/ppermute | solution.py:227
  17.6 0.5 collective-permute-start.9
  18.1 0.2 collective-permute-start.5
  18.3 2.4 %collective-permute-done.4.refs_5_ = bf16[2,32,1024]{2,1,0:T(8,128)(2,1)S(1)} collective-permute-done((bf16[2,32,1024]{2,1,0:T(8,128)(2,1)S(1)}, bf16[2,32,1024]{2,1,0:T(8,128)(2,1)S(1)}, u32[]{:S(2)}, u32[]{:S(2)}) %collective-permute-start.4) | collective-permute-done | bytes 131104 | tf_op jit(solution)/shard_map/ppermute | solution.py:227
  20.7 1.8 %collective-permute-start.6 = (bf16[2,32,1024]{2,1,0:T(8,128)(2,1)S(1)}, bf16[2,32,1024]{2,1,0:T(8,128)(2,1)S(1)}, u32[]{:S(2)}, u32[]{:S(2)}) collective-permute-start(bf16[2,32,1024]{2,1,0:T(8,128)(2,1)S(1)} %collective-permute-done.4.refs_5_), channel_id=1, source_target_pairs={{0,4},{1,5},{4,8},{5,9},{8,12},{9,13},{12,14},{13,15},{14,10},{15,... | collective-permute-start | bytes 393224 | tf_op jit(solution)/shard_map/ppermute | solution.py:227
  22.5 0.5 collective-permute-start.10
  23.1 0.9 collective-permute-done.5.refs_6_
  24.0 1.7 %collective-permute-done.6.refs_7_ = bf16[2,32,1024]{2,1,0:T(8,128)(2,1)S(1)} collective-permute-done((bf16[2,32,1024]{2,1,0:T(8,128)(2,1)S(1)}, bf16[2,32,1024]{2,1,0:T(8,128)(2,1)S(1)}, u32[]{:S(2)}, u32[]{:S(2)}) %collective-permute-start.6) | collective-permute-done | bytes 131104 | tf_op jit(solution)/shard_map/ppermute | solution.py:227
  25.7 2.8 %turn.4.refs_0_ = bf16[32,256,512]{2,1,0:T(8,128)(2,1)} custom-call(bf16[256,32,512]{2,1,0:T(8,128)(2,1)} %amp_ref.7), custom_call_target="tpu_custom_call" | custom-call | bytes 4194304 | tf_op jit(solution)/shard_map/turn/pallas_call | solution.py:105
  28.5 2.8 %turn.5.refs_0_ = bf16[32,256,512]{2,1,0:T(8,128)(2,1)} custom-call(bf16[256,32,512]{2,1,0:T(8,128)(2,1)} %amp_ref.7, bf16[32,256,512]{2,1,0:T(8,128)(2,1)} %turn.4.refs_0_), custom_call_target="tpu_custom_call", output_to_operand_aliasing={{}: (1, {})} | custom-call | bytes 4194304 | tf_op jit(solution)/shard_map/turn/pallas_call | solution.py:105
  31.4 2.8 %turn.6.refs_0_ = bf16[32,256,512]{2,1,0:T(8,128)(2,1)} custom-call(bf16[256,32,512]{2,1,0:T(8,128)(2,1)} %amp_ref.7, bf16[32,256,512]{2,1,0:T(8,128)(2,1)} %turn.5.refs_0_), custom_call_target="tpu_custom_call", output_to_operand_aliasing={{}: (1, {})} | custom-call | bytes 4194304 | tf_op jit(solution)/shard_map/turn/pallas_call | solution.py:105
  34.2 2.8 %turn.7.refs_16_ = bf16[32,256,512]{2,1,0:T(8,128)(2,1)} custom-call(bf16[256,32,512]{2,1,0:T(8,128)(2,1)} %amp_ref.7, bf16[32,256,512]{2,1,0:T(8,128)(2,1)} %turn.6.refs_0_), custom_call_target="tpu_custom_call", output_to_operand_aliasing={{}: (1, {})} | custom-call | bytes 4194304 | tf_op jit(solution)/shard_map/turn/pallas_call | solution.py:105
  37.2 38.2 %ladder.1 = (f32[8,2,32,256]{3,2,1,0:T(8,128)S(1)}, f32[8,2,32,256]{3,2,1,0:T(8,128)S(1)}) custom-call(s32[17]{0:T(128)S(1)} %stack.71.order_ref, bf16[2,32,1024]{2,1,0:T(8,128)(2,1)S(1)} %window.1.refs_0_, bf16[2,32,1024]{2,1,0:T(8,128)(2,1)S(1)} %collective-permute-done.refs_1_, bf16[2,32,1024]{2,1,0:T(8,128)(2,1)S(1)} %collective-permute-done.1.refs_2_, ...), custom_call_target="tpu_custom_call" | custom-call | flops 34359738368 | bytes 41943040 | tf_op jit(solution)/shard_map/ladder/pallas_call | solution.py:183
  75.4 0.6 collective-permute-start.15
  75.9 1.5 %collective-permute-done.15 = f32[8,2,32,256]{3,2,1,0:T(8,128)S(1)} collective-permute-done((f32[8,2,32,256]{3,2,1,0:T(8,128)S(1)}, f32[8,2,32,256]{3,2,1,0:T(8,128)S(1)}, u32[]{:S(2)}, u32[]{:S(2)}) %collective-permute-start.15) | collective-permute-done | bytes 524320 | tf_op jit(solution)/shard_map/ppermute | solution.py:255
  77.5 0.8 fusion
  78.3 6.1 %all-to-all-start = ((bf16[8,2,32,256]{3,2,1,0:T(8,128)(2,1)}), bf16[8,2,32,256]{3,2,1,0:T(8,128)(2,1)S(1)}, u32[]{:S(2)}, u32[]{:S(2)}) async-start(bf16[8,2,32,256]{3,2,1,0:T(8,128)(2,1)} %get-tuple-element.9), calls=%async_computation | async-start | bytes 524288 | tf_op jit(solution)/shard_map/all_to_all | solution.py:257
  84.3 9.4 %all-to-all-done = bf16[8,2,32,256]{3,2,1,0:T(8,128)(2,1)S(1)} async-done(((bf16[8,2,32,256]{3,2,1,0:T(8,128)(2,1)}), bf16[8,2,32,256]{3,2,1,0:T(8,128)(2,1)S(1)}, u32[]{:S(2)}, u32[]{:S(2)}) %all-to-all-start) | async-done | bytes 262176 | tf_op jit(solution)/shard_map/all_to_all | solution.py:257
  93.8 0.7 select_reduce_fusion
  (20 shorter events, 0.4 us)
Async XLA Ops:
  4.3 6.5 %collective-permute-start = (bf16[2,32,1024]{2,1,0:T(8,128)(2,1)S(1)}, bf16[2,32,1024]{2,1,0:T(8,128)(2,1)S(1)}, u32[]{:S(2)}, u32[]{:S(2)}) collective-permute-start(bf16[2,32,1024]{2,1,0:T(8,128)(2,1)S(1)} %window.1.refs_0_), channel_id=1, source_target_pairs={{0,4},{1,5},{4,8},{5,9},{8,12},{9,13},{12,14},{13,15},{14,10},{15,... | collective-permute-start | bytes 393224 | tf_op jit(solution)/shard_map/ppermute | solution.py:227
  7.4 5.2 %collective-permute-start.1 = (bf16[2,32,1024]{2,1,0:T(8,128)(2,1)S(1)}, bf16[2,32,1024]{2,1,0:T(8,128)(2,1)S(1)}, u32[]{:S(2)}, u32[]{:S(2)}) collective-permute-start(bf16[2,32,1024]{2,1,0:T(8,128)(2,1)S(1)} %window.1.refs_0_), channel_id=1, source_target_pairs={{0,2},{1,3},{4,0},{5,1},{8,4},{9,5},{12,8},{13,9},{14,12},{15,13},... | collective-permute-start | bytes 393224 | tf_op jit(solution)/shard_map/ppermute | solution.py:227
  10.8 5.0 %collective-permute-start.2 = (bf16[2,32,1024]{2,1,0:T(8,128)(2,1)S(1)}, bf16[2,32,1024]{2,1,0:T(8,128)(2,1)S(1)}, u32[]{:S(2)}, u32[]{:S(2)}) collective-permute-start(bf16[2,32,1024]{2,1,0:T(8,128)(2,1)S(1)} %collective-permute-done.refs_1_), channel_id=1, source_target_pairs={{0,4},{1,5},{4,8},{5,9},{8,12},{9,13},{12,14},{13,15},{14,10},{15,... | collective-permute-start | bytes 393224 | tf_op jit(solution)/shard_map/ppermute | solution.py:227
  12.6 5.5 %collective-permute-start.3 = (bf16[2,32,1024]{2,1,0:T(8,128)(2,1)S(1)}, bf16[2,32,1024]{2,1,0:T(8,128)(2,1)S(1)}, u32[]{:S(2)}, u32[]{:S(2)}) collective-permute-start(bf16[2,32,1024]{2,1,0:T(8,128)(2,1)S(1)} %collective-permute-done.1.refs_2_), channel_id=1, source_target_pairs={{0,2},{1,3},{4,0},{5,1},{8,4},{9,5},{12,8},{13,9},{14,12},{15,13},... | collective-permute-start | bytes 393224 | tf_op jit(solution)/shard_map/ppermute | solution.py:227
  15.8 5.0 %collective-permute-start.4 = (bf16[2,32,1024]{2,1,0:T(8,128)(2,1)S(1)}, bf16[2,32,1024]{2,1,0:T(8,128)(2,1)S(1)}, u32[]{:S(2)}, u32[]{:S(2)}) collective-permute-start(bf16[2,32,1024]{2,1,0:T(8,128)(2,1)S(1)} %collective-permute-done.2.refs_3_), channel_id=1, source_target_pairs={{0,4},{1,5},{4,8},{5,9},{8,12},{9,13},{12,14},{13,15},{14,10},{15,... | collective-permute-start | bytes 393224 | tf_op jit(solution)/shard_map/ppermute | solution.py:227
  17.6 5.0 %collective-permute-start.7 = (bf16[2,32,1024]{2,1,0:T(8,128)(2,1)S(1)}, bf16[2,32,1024]{2,1,0:T(8,128)(2,1)S(1)}, u32[]{:S(2)}, u32[]{:S(2)}) collective-permute-start(bf16[2,32,1024]{2,1,0:T(8,128)(2,1)S(1)} %window.1.refs_0_), channel_id=1, source_target_pairs={{0,1},{1,0},{2,3},{3,2},{4,5},{5,4},{6,7},{7,6},{8,9},{9,8},{10,11... | collective-permute-start | bytes 393224 | tf_op jit(solution)/shard_map/ppermute | solution.py:240
  17.6 5.0 %collective-permute-start.9 = (bf16[2,32,1024]{2,1,0:T(8,128)(2,1)S(1)}, bf16[2,32,1024]{2,1,0:T(8,128)(2,1)S(1)}, u32[]{:S(2)}, u32[]{:S(2)}) collective-permute-start(bf16[2,32,1024]{2,1,0:T(8,128)(2,1)S(1)} %collective-permute-done.1.refs_2_), channel_id=1, source_target_pairs={{0,1},{1,0},{2,3},{3,2},{4,5},{5,4},{6,7},{7,6},{8,9},{9,8},{10,11... | collective-permute-start | bytes 393224 | tf_op jit(solution)/shard_map/ppermute | solution.py:240
  18.1 5.0 %collective-permute-start.8 = (bf16[2,32,1024]{2,1,0:T(8,128)(2,1)S(1)}, bf16[2,32,1024]{2,1,0:T(8,128)(2,1)S(1)}, u32[]{:S(2)}, u32[]{:S(2)}) collective-permute-start(bf16[2,32,1024]{2,1,0:T(8,128)(2,1)S(1)} %collective-permute-done.refs_1_), channel_id=1, source_target_pairs={{0,1},{1,0},{2,3},{3,2},{4,5},{5,4},{6,7},{7,6},{8,9},{9,8},{10,11... | collective-permute-start | bytes 393224 | tf_op jit(solution)/shard_map/ppermute | solution.py:240
  18.1 5.9 %collective-permute-start.5 = (bf16[2,32,1024]{2,1,0:T(8,128)(2,1)S(1)}, bf16[2,32,1024]{2,1,0:T(8,128)(2,1)S(1)}, u32[]{:S(2)}, u32[]{:S(2)}) collective-permute-start(bf16[2,32,1024]{2,1,0:T(8,128)(2,1)S(1)} %collective-permute-done.3.refs_4_), channel_id=1, source_target_pairs={{0,2},{1,3},{4,0},{5,1},{8,4},{9,5},{12,8},{13,9},{14,12},{15,13},... | collective-permute-start | bytes 393224 | tf_op jit(solution)/shard_map/ppermute | solution.py:227
  20.7 5.0 %collective-permute-start.6 = (bf16[2,32,1024]{2,1,0:T(8,128)(2,1)S(1)}, bf16[2,32,1024]{2,1,0:T(8,128)(2,1)S(1)}, u32[]{:S(2)}, u32[]{:S(2)}) collective-permute-start(bf16[2,32,1024]{2,1,0:T(8,128)(2,1)S(1)} %collective-permute-done.4.refs_5_), channel_id=1, source_target_pairs={{0,4},{1,5},{4,8},{5,9},{8,12},{9,13},{12,14},{13,15},{14,10},{15,... | collective-permute-start | bytes 393224 | tf_op jit(solution)/shard_map/ppermute | solution.py:227
  22.5 14.6 %collective-permute-start.11 = (bf16[2,32,1024]{2,1,0:T(8,128)(2,1)S(1)}, bf16[2,32,1024]{2,1,0:T(8,128)(2,1)S(1)}, u32[]{:S(2)}, u32[]{:S(2)}) collective-permute-start(bf16[2,32,1024]{2,1,0:T(8,128)(2,1)S(1)} %collective-permute-done.3.refs_4_), channel_id=1, source_target_pairs={{0,1},{1,0},{2,3},{3,2},{4,5},{5,4},{6,7},{7,6},{8,9},{9,8},{10,11... | collective-permute-start | bytes 393224 | tf_op jit(solution)/shard_map/ppermute | solution.py:240
  22.5 14.6 %collective-permute-start.10 = (bf16[2,32,1024]{2,1,0:T(8,128)(2,1)S(1)}, bf16[2,32,1024]{2,1,0:T(8,128)(2,1)S(1)}, u32[]{:S(2)}, u32[]{:S(2)}) collective-permute-start(bf16[2,32,1024]{2,1,0:T(8,128)(2,1)S(1)} %collective-permute-done.2.refs_3_), channel_id=1, source_target_pairs={{0,1},{1,0},{2,3},{3,2},{4,5},{5,4},{6,7},{7,6},{8,9},{9,8},{10,11... | collective-permute-start | bytes 393224 | tf_op jit(solution)/shard_map/ppermute | solution.py:240
  23.1 14.1 %collective-permute-start.12 = (bf16[2,32,1024]{2,1,0:T(8,128)(2,1)S(1)}, bf16[2,32,1024]{2,1,0:T(8,128)(2,1)S(1)}, u32[]{:S(2)}, u32[]{:S(2)}) collective-permute-start(bf16[2,32,1024]{2,1,0:T(8,128)(2,1)S(1)} %collective-permute-done.4.refs_5_), channel_id=1, source_target_pairs={{0,1},{1,0},{2,3},{3,2},{4,5},{5,4},{6,7},{7,6},{8,9},{9,8},{10,11... | collective-permute-start | bytes 393224 | tf_op jit(solution)/shard_map/ppermute | solution.py:240
  24.0 13.2 %collective-permute-start.13 = (bf16[2,32,1024]{2,1,0:T(8,128)(2,1)S(1)}, bf16[2,32,1024]{2,1,0:T(8,128)(2,1)S(1)}, u32[]{:S(2)}, u32[]{:S(2)}) collective-permute-start(bf16[2,32,1024]{2,1,0:T(8,128)(2,1)S(1)} %collective-permute-done.5.refs_6_), channel_id=1, source_target_pairs={{0,1},{1,0},{2,3},{3,2},{4,5},{5,4},{6,7},{7,6},{8,9},{9,8},{10,11... | collective-permute-start | bytes 393224 | tf_op jit(solution)/shard_map/ppermute | solution.py:240
  25.7 11.5 %collective-permute-start.14 = (bf16[2,32,1024]{2,1,0:T(8,128)(2,1)S(1)}, bf16[2,32,1024]{2,1,0:T(8,128)(2,1)S(1)}, u32[]{:S(2)}, u32[]{:S(2)}) collective-permute-start(bf16[2,32,1024]{2,1,0:T(8,128)(2,1)S(1)} %collective-permute-done.6.refs_7_), channel_id=1, source_target_pairs={{0,1},{1,0},{2,3},{3,2},{4,5},{5,4},{6,7},{7,6},{8,9},{9,8},{10,11... | collective-permute-start | bytes 393224 | tf_op jit(solution)/shard_map/ppermute | solution.py:240
  75.4 2.1 %collective-permute-start.15 = (f32[8,2,32,256]{3,2,1,0:T(8,128)S(1)}, f32[8,2,32,256]{3,2,1,0:T(8,128)S(1)}, u32[]{:S(2)}, u32[]{:S(2)}) collective-permute-start(f32[8,2,32,256]{3,2,1,0:T(8,128)S(1)} %get-tuple-element.8), channel_id=1, source_target_pairs={{0,1},{1,0},{2,3},{3,2},{4,5},{5,4},{6,7},{7,6},{8,9},{9,8},{10,11... | collective-permute-start | bytes 1572872 | tf_op jit(solution)/shard_map/ppermute | solution.py:255
  78.3 15.5 %all-to-all-start = ((bf16[8,2,32,256]{3,2,1,0:T(8,128)(2,1)}), bf16[8,2,32,256]{3,2,1,0:T(8,128)(2,1)S(1)}, u32[]{:S(2)}, u32[]{:S(2)}) async-start(bf16[8,2,32,256]{3,2,1,0:T(8,128)(2,1)} %get-tuple-element.9), calls=%async_computation | async-start | bytes 524288 | tf_op jit(solution)/shard_map/all_to_all | solution.py:257

commit v4 on v3

--- a/solution.py
+++ b/solution.py
@@ -139,8 +139,7 @@
                 copy.start()
         return max(after, min(upto, steps))
 
-    issued = issue(0, slots - 1)
-    total[...] = jnp.zeros_like(total)
+    issued = issue(0, min(slots, 3))
     for i in range(pieces):
         start = pl.multiple_of(order_ref[i] * own, own)
         for a in range(A_WIN):
@@ -158,7 +157,8 @@
                 half[c % 2, a * pairs : (a + 1) * pairs, :] = jnp.dot(
                     amps[c % slots], window[a], preferred_element_type=jnp.float32
                 ).astype(half.dtype)
-            total[...] += jnp.dot(half[c % 2], chols[c % slots], preferred_element_type=jnp.float32)
+            added = jnp.dot(half[c % 2], chols[c % slots], preferred_element_type=jnp.float32)
+            total[...] = total[...] + added if c else added
         first += size
         size = min(GROUP, first)
 

time: 94.8 us -> 94.9 us (level)
  no operation moved by 1% of the time
where the time goes in v4:
time: 94.9 us; the launch traced here: 94.6 us
  Pallas kernels  53.8 us (57%)
  waiting for transfers between devices  22.4 us (24%)
  starting transfers between devices  16.7 us (18%)
  other arithmetic  1.54 us (2%)
    pallas_call x1, Pallas kernels, ladder_of(): pl.pallas_call(functools.partial(ladder_kernel, pieces=len(pieces), slots...  38.2 us
    ppermute x7, waiting for transfers between devices, hop(): return lax.ppermute(piece, 'col', along(step))  11.4 us
    pallas_call x4, Pallas kernels, turn(): pl.pallas_call(functools.partial(turn_kernel, first=part * tile), out_sha...  11.3 us
    all_to_all x1, waiting for transfers between devices, part(): lax.all_to_all(summed.astype(jnp.bfloat16), 'col', 0, 0, tiled=True, axis...  9.45 us
    ppermute x7, starting transfers between devices, hop(): return lax.ppermute(piece, 'col', along(step))  8.96 us
    all_to_all x1, starting transfers between devices, part(): lax.all_to_all(summed.astype(jnp.bfloat16), 'col', 0, 0, tiled=True, axis...  6.05 us
    pallas_call x1, Pallas kernels, window_of(): pl.pallas_call(window_kernel, out_shape=jax.ShapeDtypeStruct((A_WIN, own,...  4.24 us
  transfers between devices with their start and end apart: 17, of which 7 were waited for; matrix products, arithmetic and copies ran while one was open for 0% of the time, Pallas kernels for 12%

profile of v4, /device:TPU:0, one launch (start us, length us, event | category | flops | bytes accessed | tf_op | source)
XLA Modules:
  0.0 94.6 jit_solution(7714044262075860648)
XLA Ops:
  0.0 4.2 %window.1.refs_0_ = bf16[2,32,1024]{2,1,0:T(8,128)(2,1)S(1)} custom-call(bf16[32,1024,512]{2,1,0:T(8,128)(2,1)} %refs_17_.1), custom_call_target="tpu_custom_call" | custom-call | bytes 8388608 | tf_op jit(solution)/shard_map/window/pallas_call | solution.py:59
  4.3 3.1 %collective-permute-start = (bf16[2,32,1024]{2,1,0:T(8,128)(2,1)S(1)}, bf16[2,32,1024]{2,1,0:T(8,128)(2,1)S(1)}, u32[]{:S(2)}, u32[]{:S(2)}) collective-permute-start(bf16[2,32,1024]{2,1,0:T(8,128)(2,1)S(1)} %window.1.refs_0_), channel_id=1, source_target_pairs={{0,4},{1,5},{4,8},{5,9},{8,12},{9,13},{12,14},{13,15},{14,10},{15,... | collective-permute-start | bytes 393224 | tf_op jit(solution)/shard_map/ppermute | solution.py:227
  7.4 3.4 %collective-permute-done.refs_1_ = bf16[2,32,1024]{2,1,0:T(8,128)(2,1)S(1)} collective-permute-done((bf16[2,32,1024]{2,1,0:T(8,128)(2,1)S(1)}, bf16[2,32,1024]{2,1,0:T(8,128)(2,1)S(1)}, u32[]{:S(2)}, u32[]{:S(2)}) %collective-permute-start) | collective-permute-done | bytes 131104 | tf_op jit(solution)/shard_map/ppermute | solution.py:227
  10.8 1.8 %collective-permute-start.2 = (bf16[2,32,1024]{2,1,0:T(8,128)(2,1)S(1)}, bf16[2,32,1024]{2,1,0:T(8,128)(2,1)S(1)}, u32[]{:S(2)}, u32[]{:S(2)}) collective-permute-start(bf16[2,32,1024]{2,1,0:T(8,128)(2,1)S(1)} %collective-permute-done.refs_1_), channel_id=1, source_target_pairs={{0,4},{1,5},{4,8},{5,9},{8,12},{9,13},{12,14},{13,15},{14,10},{15,... | collective-permute-start | bytes 393224 | tf_op jit(solution)/shard_map/ppermute | solution.py:227
  12.8 2.9 %collective-permute-done.2.refs_3_ = bf16[2,32,1024]{2,1,0:T(8,128)(2,1)S(1)} collective-permute-done((bf16[2,32,1024]{2,1,0:T(8,128)(2,1)S(1)}, bf16[2,32,1024]{2,1,0:T(8,128)(2,1)S(1)}, u32[]{:S(2)}, u32[]{:S(2)}) %collective-permute-start.2) | collective-permute-done | bytes 131104 | tf_op jit(solution)/shard_map/ppermute | solution.py:227
  15.8 1.8 %collective-permute-start.4 = (bf16[2,32,1024]{2,1,0:T(8,128)(2,1)S(1)}, bf16[2,32,1024]{2,1,0:T(8,128)(2,1)S(1)}, u32[]{:S(2)}, u32[]{:S(2)}) collective-permute-start(bf16[2,32,1024]{2,1,0:T(8,128)(2,1)S(1)} %collective-permute-done.2.refs_3_), channel_id=1, source_target_pairs={{0,4},{1,5},{4,8},{5,9},{8,12},{9,13},{12,14},{13,15},{14,10},{15,... | collective-permute-start | bytes 393224 | tf_op jit(solution)/shard_map/ppermute | solution.py:227
  17.6 0.5 collective-permute-start.9
  18.1 0.2 collective-permute-start.5
  18.3 2.4 %collective-permute-done.4.refs_5_ = bf16[2,32,1024]{2,1,0:T(8,128)(2,1)S(1)} collective-permute-done((bf16[2,32,1024]{2,1,0:T(8,128)(2,1)S(1)}, bf16[2,32,1024]{2,1,0:T(8,128)(2,1)S(1)}, u32[]{:S(2)}, u32[]{:S(2)}) %collective-permute-start.4) | collective-permute-done | bytes 131104 | tf_op jit(solution)/shard_map/ppermute | solution.py:227
  20.7 1.8 %collective-permute-start.6 = (bf16[2,32,1024]{2,1,0:T(8,128)(2,1)S(1)}, bf16[2,32,1024]{2,1,0:T(8,128)(2,1)S(1)}, u32[]{:S(2)}, u32[]{:S(2)}) collective-permute-start(bf16[2,32,1024]{2,1,0:T(8,128)(2,1)S(1)} %collective-permute-done.4.refs_5_), channel_id=1, source_target_pairs={{0,4},{1,5},{4,8},{5,9},{8,12},{9,13},{12,14},{13,15},{14,10},{15,... | collective-permute-start | bytes 393224 | tf_op jit(solution)/shard_map/ppermute | solution.py:227
  22.5 0.5 collective-permute-start.10
  23.1 0.9 collective-permute-done.5.refs_6_
  24.0 1.7 %collective-permute-done.6.refs_7_ = bf16[2,32,1024]{2,1,0:T(8,128)(2,1)S(1)} collective-permute-done((bf16[2,32,1024]{2,1,0:T(8,128)(2,1)S(1)}, bf16[2,32,1024]{2,1,0:T(8,128)(2,1)S(1)}, u32[]{:S(2)}, u32[]{:S(2)}) %collective-permute-start.6) | collective-permute-done | bytes 131104 | tf_op jit(solution)/shard_map/ppermute | solution.py:227
  25.7 2.8 %turn.4.refs_0_ = bf16[32,256,512]{2,1,0:T(8,128)(2,1)} custom-call(bf16[256,32,512]{2,1,0:T(8,128)(2,1)} %amp_ref.7), custom_call_target="tpu_custom_call" | custom-call | bytes 4194304 | tf_op jit(solution)/shard_map/turn/pallas_call | solution.py:105
  28.5 2.8 %turn.5.refs_0_ = bf16[32,256,512]{2,1,0:T(8,128)(2,1)} custom-call(bf16[256,32,512]{2,1,0:T(8,128)(2,1)} %amp_ref.7, bf16[32,256,512]{2,1,0:T(8,128)(2,1)} %turn.4.refs_0_), custom_call_target="tpu_custom_call", output_to_operand_aliasing={{}: (1, {})} | custom-call | bytes 4194304 | tf_op jit(solution)/shard_map/turn/pallas_call | solution.py:105
  31.4 2.8 %turn.6.refs_0_ = bf16[32,256,512]{2,1,0:T(8,128)(2,1)} custom-call(bf16[256,32,512]{2,1,0:T(8,128)(2,1)} %amp_ref.7, bf16[32,256,512]{2,1,0:T(8,128)(2,1)} %turn.5.refs_0_), custom_call_target="tpu_custom_call", output_to_operand_aliasing={{}: (1, {})} | custom-call | bytes 4194304 | tf_op jit(solution)/shard_map/turn/pallas_call | solution.py:105
  34.2 2.8 %turn.7.refs_16_ = bf16[32,256,512]{2,1,0:T(8,128)(2,1)} custom-call(bf16[256,32,512]{2,1,0:T(8,128)(2,1)} %amp_ref.7, bf16[32,256,512]{2,1,0:T(8,128)(2,1)} %turn.6.refs_0_), custom_call_target="tpu_custom_call", output_to_operand_aliasing={{}: (1, {})} | custom-call | bytes 4194304 | tf_op jit(solution)/shard_map/turn/pallas_call | solution.py:105
  37.2 38.2 %ladder.1 = (f32[8,2,32,256]{3,2,1,0:T(8,128)S(1)}, f32[8,2,32,256]{3,2,1,0:T(8,128)S(1)}) custom-call(s32[17]{0:T(128)S(1)} %stack.71.order_ref, bf16[2,32,1024]{2,1,0:T(8,128)(2,1)S(1)} %window.1.refs_0_, bf16[2,32,1024]{2,1,0:T(8,128)(2,1)S(1)} %collective-permute-done.refs_1_, bf16[2,32,1024]{2,1,0:T(8,128)(2,1)S(1)} %collective-permute-done.1.refs_2_, ...), custom_call_target="tpu_custom_call" | custom-call | flops 34359738368 | bytes 41943040 | tf_op jit(solution)/shard_map/ladder/pallas_call | solution.py:183
  75.5 0.6 collective-permute-start.15
  76.0 1.5 %collective-permute-done.15 = f32[8,2,32,256]{3,2,1,0:T(8,128)S(1)} collective-permute-done((f32[8,2,32,256]{3,2,1,0:T(8,128)S(1)}, f32[8,2,32,256]{3,2,1,0:T(8,128)S(1)}, u32[]{:S(2)}, u32[]{:S(2)}) %collective-permute-start.15) | collective-permute-done | bytes 524320 | tf_op jit(solution)/shard_map/ppermute | solution.py:255
  77.6 0.8 fusion
  78.4 6.1 %all-to-all-start = ((bf16[8,2,32,256]{3,2,1,0:T(8,128)(2,1)}), bf16[8,2,32,256]{3,2,1,0:T(8,128)(2,1)S(1)}, u32[]{:S(2)}, u32[]{:S(2)}) async-start(bf16[8,2,32,256]{3,2,1,0:T(8,128)(2,1)} %get-tuple-element.9), calls=%async_computation | async-start | bytes 524288 | tf_op jit(solution)/shard_map/all_to_all | solution.py:257
  84.4 9.4 %all-to-all-done = bf16[8,2,32,256]{3,2,1,0:T(8,128)(2,1)S(1)} async-done(((bf16[8,2,32,256]{3,2,1,0:T(8,128)(2,1)}), bf16[8,2,32,256]{3,2,1,0:T(8,128)(2,1)S(1)}, u32[]{:S(2)}, u32[]{:S(2)}) %all-to-all-start) | async-done | bytes 262176 | tf_op jit(solution)/shard_map/all_to_all | solution.py:257
  93.9 0.7 select_reduce_fusion
  (20 shorter events, 0.4 us)
Async XLA Ops:
  4.3 6.5 %collective-permute-start = (bf16[2,32,1024]{2,1,0:T(8,128)(2,1)S(1)}, bf16[2,32,1024]{2,1,0:T(8,128)(2,1)S(1)}, u32[]{:S(2)}, u32[]{:S(2)}) collective-permute-start(bf16[2,32,1024]{2,1,0:T(8,128)(2,1)S(1)} %window.1.refs_0_), channel_id=1, source_target_pairs={{0,4},{1,5},{4,8},{5,9},{8,12},{9,13},{12,14},{13,15},{14,10},{15,... | collective-permute-start | bytes 393224 | tf_op jit(solution)/shard_map/ppermute | solution.py:227
  7.4 5.2 %collective-permute-start.1 = (bf16[2,32,1024]{2,1,0:T(8,128)(2,1)S(1)}, bf16[2,32,1024]{2,1,0:T(8,128)(2,1)S(1)}, u32[]{:S(2)}, u32[]{:S(2)}) collective-permute-start(bf16[2,32,1024]{2,1,0:T(8,128)(2,1)S(1)} %window.1.refs_0_), channel_id=1, source_target_pairs={{0,2},{1,3},{4,0},{5,1},{8,4},{9,5},{12,8},{13,9},{14,12},{15,13},... | collective-permute-start | bytes 393224 | tf_op jit(solution)/shard_map/ppermute | solution.py:227
  10.8 5.0 %collective-permute-start.2 = (bf16[2,32,1024]{2,1,0:T(8,128)(2,1)S(1)}, bf16[2,32,1024]{2,1,0:T(8,128)(2,1)S(1)}, u32[]{:S(2)}, u32[]{:S(2)}) collective-permute-start(bf16[2,32,1024]{2,1,0:T(8,128)(2,1)S(1)} %collective-permute-done.refs_1_), channel_id=1, source_target_pairs={{0,4},{1,5},{4,8},{5,9},{8,12},{9,13},{12,14},{13,15},{14,10},{15,... | collective-permute-start | bytes 393224 | tf_op jit(solution)/shard_map/ppermute | solution.py:227
  12.6 5.5 %collective-permute-start.3 = (bf16[2,32,1024]{2,1,0:T(8,128)(2,1)S(1)}, bf16[2,32,1024]{2,1,0:T(8,128)(2,1)S(1)}, u32[]{:S(2)}, u32[]{:S(2)}) collective-permute-start(bf16[2,32,1024]{2,1,0:T(8,128)(2,1)S(1)} %collective-permute-done.1.refs_2_), channel_id=1, source_target_pairs={{0,2},{1,3},{4,0},{5,1},{8,4},{9,5},{12,8},{13,9},{14,12},{15,13},... | collective-permute-start | bytes 393224 | tf_op jit(solution)/shard_map/ppermute | solution.py:227
  15.8 5.0 %collective-permute-start.4 = (bf16[2,32,1024]{2,1,0:T(8,128)(2,1)S(1)}, bf16[2,32,1024]{2,1,0:T(8,128)(2,1)S(1)}, u32[]{:S(2)}, u32[]{:S(2)}) collective-permute-start(bf16[2,32,1024]{2,1,0:T(8,128)(2,1)S(1)} %collective-permute-done.2.refs_3_), channel_id=1, source_target_pairs={{0,4},{1,5},{4,8},{5,9},{8,12},{9,13},{12,14},{13,15},{14,10},{15,... | collective-permute-start | bytes 393224 | tf_op jit(solution)/shard_map/ppermute | solution.py:227
  17.6 5.0 %collective-permute-start.7 = (bf16[2,32,1024]{2,1,0:T(8,128)(2,1)S(1)}, bf16[2,32,1024]{2,1,0:T(8,128)(2,1)S(1)}, u32[]{:S(2)}, u32[]{:S(2)}) collective-permute-start(bf16[2,32,1024]{2,1,0:T(8,128)(2,1)S(1)} %window.1.refs_0_), channel_id=1, source_target_pairs={{0,1},{1,0},{2,3},{3,2},{4,5},{5,4},{6,7},{7,6},{8,9},{9,8},{10,11... | collective-permute-start | bytes 393224 | tf_op jit(solution)/shard_map/ppermute | solution.py:240
  17.6 5.0 %collective-permute-start.9 = (bf16[2,32,1024]{2,1,0:T(8,128)(2,1)S(1)}, bf16[2,32,1024]{2,1,0:T(8,128)(2,1)S(1)}, u32[]{:S(2)}, u32[]{:S(2)}) collective-permute-start(bf16[2,32,1024]{2,1,0:T(8,128)(2,1)S(1)} %collective-permute-done.1.refs_2_), channel_id=1, source_target_pairs={{0,1},{1,0},{2,3},{3,2},{4,5},{5,4},{6,7},{7,6},{8,9},{9,8},{10,11... | collective-permute-start | bytes 393224 | tf_op jit(solution)/shard_map/ppermute | solution.py:240
  18.1 5.0 %collective-permute-start.8 = (bf16[2,32,1024]{2,1,0:T(8,128)(2,1)S(1)}, bf16[2,32,1024]{2,1,0:T(8,128)(2,1)S(1)}, u32[]{:S(2)}, u32[]{:S(2)}) collective-permute-start(bf16[2,32,1024]{2,1,0:T(8,128)(2,1)S(1)} %collective-permute-done.refs_1_), channel_id=1, source_target_pairs={{0,1},{1,0},{2,3},{3,2},{4,5},{5,4},{6,7},{7,6},{8,9},{9,8},{10,11... | collective-permute-start | bytes 393224 | tf_op jit(solution)/shard_map/ppermute | solution.py:240
  18.1 5.9 %collective-permute-start.5 = (bf16[2,32,1024]{2,1,0:T(8,128)(2,1)S(1)}, bf16[2,32,1024]{2,1,0:T(8,128)(2,1)S(1)}, u32[]{:S(2)}, u32[]{:S(2)}) collective-permute-start(bf16[2,32,1024]{2,1,0:T(8,128)(2,1)S(1)} %collective-permute-done.3.refs_4_), channel_id=1, source_target_pairs={{0,2},{1,3},{4,0},{5,1},{8,4},{9,5},{12,8},{13,9},{14,12},{15,13},... | collective-permute-start | bytes 393224 | tf_op jit(solution)/shard_map/ppermute | solution.py:227
  20.7 5.0 %collective-permute-start.6 = (bf16[2,32,1024]{2,1,0:T(8,128)(2,1)S(1)}, bf16[2,32,1024]{2,1,0:T(8,128)(2,1)S(1)}, u32[]{:S(2)}, u32[]{:S(2)}) collective-permute-start(bf16[2,32,1024]{2,1,0:T(8,128)(2,1)S(1)} %collective-permute-done.4.refs_5_), channel_id=1, source_target_pairs={{0,4},{1,5},{4,8},{5,9},{8,12},{9,13},{12,14},{13,15},{14,10},{15,... | collective-permute-start | bytes 393224 | tf_op jit(solution)/shard_map/ppermute | solution.py:227
  22.5 14.6 %collective-permute-start.11 = (bf16[2,32,1024]{2,1,0:T(8,128)(2,1)S(1)}, bf16[2,32,1024]{2,1,0:T(8,128)(2,1)S(1)}, u32[]{:S(2)}, u32[]{:S(2)}) collective-permute-start(bf16[2,32,1024]{2,1,0:T(8,128)(2,1)S(1)} %collective-permute-done.3.refs_4_), channel_id=1, source_target_pairs={{0,1},{1,0},{2,3},{3,2},{4,5},{5,4},{6,7},{7,6},{8,9},{9,8},{10,11... | collective-permute-start | bytes 393224 | tf_op jit(solution)/shard_map/ppermute | solution.py:240
  22.5 14.6 %collective-permute-start.10 = (bf16[2,32,1024]{2,1,0:T(8,128)(2,1)S(1)}, bf16[2,32,1024]{2,1,0:T(8,128)(2,1)S(1)}, u32[]{:S(2)}, u32[]{:S(2)}) collective-permute-start(bf16[2,32,1024]{2,1,0:T(8,128)(2,1)S(1)} %collective-permute-done.2.refs_3_), channel_id=1, source_target_pairs={{0,1},{1,0},{2,3},{3,2},{4,5},{5,4},{6,7},{7,6},{8,9},{9,8},{10,11... | collective-permute-start | bytes 393224 | tf_op jit(solution)/shard_map/ppermute | solution.py:240
  23.1 14.1 %collective-permute-start.12 = (bf16[2,32,1024]{2,1,0:T(8,128)(2,1)S(1)}, bf16[2,32,1024]{2,1,0:T(8,128)(2,1)S(1)}, u32[]{:S(2)}, u32[]{:S(2)}) collective-permute-start(bf16[2,32,1024]{2,1,0:T(8,128)(2,1)S(1)} %collective-permute-done.4.refs_5_), channel_id=1, source_target_pairs={{0,1},{1,0},{2,3},{3,2},{4,5},{5,4},{6,7},{7,6},{8,9},{9,8},{10,11... | collective-permute-start | bytes 393224 | tf_op jit(solution)/shard_map/ppermute | solution.py:240
  24.0 13.2 %collective-permute-start.13 = (bf16[2,32,1024]{2,1,0:T(8,128)(2,1)S(1)}, bf16[2,32,1024]{2,1,0:T(8,128)(2,1)S(1)}, u32[]{:S(2)}, u32[]{:S(2)}) collective-permute-start(bf16[2,32,1024]{2,1,0:T(8,128)(2,1)S(1)} %collective-permute-done.5.refs_6_), channel_id=1, source_target_pairs={{0,1},{1,0},{2,3},{3,2},{4,5},{5,4},{6,7},{7,6},{8,9},{9,8},{10,11... | collective-permute-start | bytes 393224 | tf_op jit(solution)/shard_map/ppermute | solution.py:240
  25.7 11.5 %collective-permute-start.14 = (bf16[2,32,1024]{2,1,0:T(8,128)(2,1)S(1)}, bf16[2,32,1024]{2,1,0:T(8,128)(2,1)S(1)}, u32[]{:S(2)}, u32[]{:S(2)}) collective-permute-start(bf16[2,32,1024]{2,1,0:T(8,128)(2,1)S(1)} %collective-permute-done.6.refs_7_), channel_id=1, source_target_pairs={{0,1},{1,0},{2,3},{3,2},{4,5},{5,4},{6,7},{7,6},{8,9},{9,8},{10,11... | collective-permute-start | bytes 393224 | tf_op jit(solution)/shard_map/ppermute | solution.py:240
  75.5 2.1 %collective-permute-start.15 = (f32[8,2,32,256]{3,2,1,0:T(8,128)S(1)}, f32[8,2,32,256]{3,2,1,0:T(8,128)S(1)}, u32[]{:S(2)}, u32[]{:S(2)}) collective-permute-start(f32[8,2,32,256]{3,2,1,0:T(8,128)S(1)} %get-tuple-element.8), channel_id=1, source_target_pairs={{0,1},{1,0},{2,3},{3,2},{4,5},{5,4},{6,7},{7,6},{8,9},{9,8},{10,11... | collective-permute-start | bytes 1572872 | tf_op jit(solution)/shard_map/ppermute | solution.py:255
  78.4 15.5 %all-to-all-start = ((bf16[8,2,32,256]{3,2,1,0:T(8,128)(2,1)}), bf16[8,2,32,256]{3,2,1,0:T(8,128)(2,1)S(1)}, u32[]{:S(2)}, u32[]{:S(2)}) async-start(bf16[8,2,32,256]{3,2,1,0:T(8,128)(2,1)} %get-tuple-element.9), calls=%async_computation | async-start | bytes 524288 | tf_op jit(solution)/shard_map/all_to_all | solution.py:257
